TPU v7x, 256 devices: a whole 4x4x8 slice. The times are simulated.
256 devices in a mesh: row: 32 (over y, x, z_hi), col: 8 (over z_lo, core).
Axes of the slice: x: 4, y: 4, z: 8 (z_hi: 2, z_lo: 4; z = z_hi * 4 + z_lo), core: 2. Of those that a mesh axis runs over, the one named last changes fastest.
Arguments:
- density: bfloat16 [6144, 5, 64, 64], P(('row', 'col')), may hold values from -0.29882812 to 0.29882812
- margin: bfloat16 [6144, 5, 64, 64], P(('row', 'col')), may hold values from -6 to 6
- potential: float32 [32, 32, 2048], P('row', None, 'col'), may hold values from -6 to 6
- basis_values: bfloat16 [2048, 8, 64, 1024], P(('row', 'col')), may hold values from -1.1953125 to 1.1953125
- pair_owner: int32 [6144, 5, 1], P(('row', 'col')), may hold values from 0 to 255; in each aligned block of 120 rows (0 to 119, 120 to 239, ..., all dimensions but the last counted through in order) at most 2 rows name the same one
- pair_box: int32 [6144, 5], P(('row', 'col')), may hold values from 0 to 7
- pair_slots: int32 [6144, 5, 2], P(('row', 'col')), may hold values from 0 to 7
Outputs:
- density_grid: float32 [32, 32, 2048], P(None, 'row', 'col')
- ks_blocks: bfloat16 [6144, 5, 64, 64], P(('row', 'col'))
- margin_product: bfloat16 [6144, 5, 64, 64], P(('row', 'col'))
Inputs may be any that keep to these rules, and one draw needn't show every extreme that they name: `pair_owner`: among the pairs of one device's atoms, at most 2 name the same owner, and exactly 2 do for some owner.
All inputs are finite; a program needn't handle non-finite values.
Results may differ from a plain program's by a relative error of at most 0.0049.
Values may be sent and summed in bfloat16 or wider, within the bound.
A program may use at most 128 MiB of HBM per device.

v0:
```python
import jax
import jax.numpy as jnp
from jax import lax
from jax.sharding import PartitionSpec as P

HALF = 2


def padded(array, sides, width):
    for axis, dim in sides:
        size, length = (lax.axis_size(axis), array.shape[dim])
        up = [(i, (i + 1) % size) for i in range(size)]
        down = [(j, i) for i, j in up]
        last = lax.slice_in_dim(array, length - width, length, axis=dim)
        first = lax.slice_in_dim(array, 0, width, axis=dim)
        before = lax.ppermute(last, axis, up)
        after = lax.ppermute(first, axis, down)
        array = jnp.concatenate([before, array, after], axis=dim)
    return array


def local(density, margin, potential, basis_values, pair_owner, pair_box, pair_slots):
    atoms_here = density.shape[0]
    offsets = density.shape[1]
    block_width = density.shape[2]
    extended = padded(margin, ((("row", "col"), 0),), HALF)
    columns = []
    for offset in range(offsets):
        lowest = max(0, offset - HALF)
        highest = min(offsets - 1, offset + HALF)
        left_blocks = density[:, lowest : highest + 1]
        right_blocks = jnp.stack(
            [
                extended[middle : middle + atoms_here, offset - middle + HALF]
                for middle in range(lowest, highest + 1)
            ],
            axis=1,
        )
        columns.append(
            jnp.einsum(
                "amik,amkj->aij", left_blocks, right_blocks, preferred_element_type=jnp.float32
            )
        )
    margin_product = jnp.stack(columns, axis=1).astype(jnp.bfloat16)
    pencil = lax.all_to_all(potential, "row", split_axis=1, concat_axis=0, tiled=True)
    tasks_here = basis_values.shape[0]
    box_points = basis_values.shape[3]
    box_potential = pencil.reshape(tasks_here, box_points)
    pair_count = atoms_here * offsets
    row_count = lax.axis_size("row")
    col_count = lax.axis_size("col")
    devices = row_count * col_count
    capacity = max(2, (2 * pair_count + devices - 1) // devices)
    slot_total = devices * capacity
    square = block_width * block_width
    owners = pair_owner.reshape(pair_count)
    targets = (owners[:, None] == jnp.arange(devices, dtype=jnp.int32)[None, :]).astype(jnp.int32)
    earlier = jnp.cumsum(targets, axis=0) - targets
    places = owners * capacity + jnp.sum(earlier * targets, axis=1)
    flat_blocks = density.reshape(pair_count, square)
    outgoing = jnp.zeros((slot_total, square), jnp.bfloat16).at[places].set(flat_blocks)
    outgoing = outgoing.reshape(row_count, col_count, capacity, square)
    labels = (
        jnp.stack(
            [
                pair_box.reshape(pair_count),
                pair_slots[..., 0].reshape(pair_count),
                pair_slots[..., 1].reshape(pair_count),
            ],
            axis=1,
        )
        .astype(jnp.float32)
        .astype(jnp.bfloat16)
    )
    outgoing_labels = jnp.zeros((slot_total, 3), jnp.bfloat16).at[places].set(labels)
    outgoing_labels = outgoing_labels.reshape(row_count, col_count, capacity, 3)
    arrived, arrived_labels = (
        lax.all_to_all(
            lax.all_to_all(outgoing, "row", split_axis=0, concat_axis=0, tiled=True),
            "col",
            split_axis=1,
            concat_axis=1,
            tiled=True,
        ),
        lax.all_to_all(
            lax.all_to_all(outgoing_labels, "row", split_axis=0, concat_axis=0, tiled=True),
            "col",
            split_axis=1,
            concat_axis=1,
            tiled=True,
        ),
    )
    group_count = 8
    per_group = slot_total // group_count
    arrived = arrived.reshape(group_count, per_group, block_width, block_width)
    tags_in = arrived_labels.astype(jnp.int32).reshape(group_count, per_group, 3)
    task_range = jnp.arange(tasks_here, dtype=jnp.int32)

    def handle(packet):
        blocks, tags = packet
        task_ids = tags[:, 0]
        first_basis = basis_values[task_ids, tags[:, 1]]
        second_basis = basis_values[task_ids, tags[:, 2]]
        weighted = jnp.einsum(
            "sij,sjg->sig", blocks, second_basis, preferred_element_type=jnp.float32
        )
        contrib = jnp.sum(first_basis.astype(jnp.float32) * weighted, axis=1)
        scaled = (first_basis.astype(jnp.float32) * box_potential[task_ids][:, None, :]).astype(
            jnp.bfloat16
        )
        matrix = jnp.einsum(
            "sig,sjg->sij", scaled, second_basis, preferred_element_type=jnp.float32
        )
        selector = (task_ids[:, None] == task_range[None, :]).astype(jnp.float32)
        grid_part = jnp.dot(selector.T, contrib, precision=lax.Precision.HIGHEST)
        return (matrix.astype(jnp.bfloat16), grid_part)

    matrices, grid_parts = lax.map(handle, (arrived, tags_in))
    density_grid = jnp.sum(grid_parts, axis=0).reshape(pencil.shape)
    results = matrices.reshape(row_count, col_count, capacity, square)
    returned = lax.all_to_all(
        lax.all_to_all(results, "row", split_axis=0, concat_axis=0, tiled=True),
        "col",
        split_axis=1,
        concat_axis=1,
        tiled=True,
    )
    ks_blocks = returned.reshape(slot_total, square)[places].reshape(
        atoms_here, offsets, block_width, block_width
    )
    return (density_grid, ks_blocks, margin_product)


def solution(mesh):
    placed = (
        P(("row", "col"), None, None, None),
        P(("row", "col"), None, None, None),
        P("row", None, "col"),
        P(("row", "col"), None, None, None),
        P(("row", "col"), None, None),
        P(("row", "col"), None),
        P(("row", "col"), None, None),
    )
    return jax.shard_map(
        local,
        mesh=mesh,
        in_specs=placed,
        out_specs=(
            P(None, "row", "col"),
            P(("row", "col"), None, None, None),
            P(("row", "col"), None, None, None),
        ),
        check_vma=False,
    )
```

profile of v0, /device:TPU:33, one launch (start us, length us, event | category | flops | bytes accessed | tf_op | source)
XLA Modules:
  0.0 867.5 jit_solution(9671600431047959758)
XLA Ops:
  6.4 23.6 %all_to_all.39 = bf16[32,8,2,3]{1,2,3,0:T(2,128)(2,1)S(1)} all-to-all(bf16[32,8,2,3]{1,2,3,0:T(2,128)(2,1)S(1)} %copy.96), channel_id=1, replica_groups=mesh['row'=32,'col'=8] {'row'}, dimensions={0} | all-to-all | bytes 6144 | tf_op jit(solution)/shard_map/all_to_all | solution.py:86
  44.5 7.6 reshape.80
  57.8 100.1 %all-to-all-done.3 = bf16[32,8,2,4096]{3,2,1,0:T(2,128)(2,1)} async-done(((bf16[32,8,2,4096]{3,2,1,0:T(2,128)(2,1)}), bf16[32,8,2,4096]{3,2,1,0:T(2,128)(2,1)}, u32[]{:S(2)}, u32[]{:S(2)}) %all-to-all-start.3) | async-done | bytes 4194336 | tf_op jit(solution)/shard_map/all_to_all | solution.py:79
  161.9 9.9 %copy.101 = bf16[32,8,2,4096]{3,2,0,1:T(2,128)(2,1)} copy(bf16[32,8,2,4096]{3,2,1,0:T(2,128)(2,1)} %all-to-all-done.3) | data formatting | bytes 8388608 | tf_op jit(solution)/shard_map/all_to_all | solution.py:79
  172.9 16.8 %all-to-all-start.4 = ((bf16[32,8,2,4096]{3,2,0,1:T(2,128)(2,1)}), bf16[32,8,2,4096]{3,2,0,1:T(2,128)(2,1)}, u32[]{:S(2)}, u32[]{:S(2)}) async-start(bf16[32,8,2,4096]{3,2,0,1:T(2,128)(2,1)} %copy.101), calls=%async_computation.4 | async-start | bytes 8388608 | tf_op jit(solution)/shard_map/all_to_all | solution.py:78
  190.3 89.9 %all-to-all-done.4 = bf16[32,8,2,4096]{3,2,0,1:T(2,128)(2,1)} async-done(((bf16[32,8,2,4096]{3,2,0,1:T(2,128)(2,1)}), bf16[32,8,2,4096]{3,2,0,1:T(2,128)(2,1)}, u32[]{:S(2)}, u32[]{:S(2)}) %all-to-all-start.4) | async-done | bytes 4194336 | tf_op jit(solution)/shard_map/all_to_all | solution.py:78
  280.2 10.1 %copy.102 = bf16[32,8,2,4096]{3,2,1,0:T(2,128)(2,1)} copy(bf16[32,8,2,4096]{3,2,0,1:T(2,128)(2,1)} %all-to-all-done.4) | data formatting | bytes 8388608 | tf_op jit(solution)/shard_map/all_to_all | solution.py:78
  290.3 14.2 %reshape.81 = bf16[8,64,64,64]{3,2,1,0:T(8,128)(2,1)} reshape(bf16[32,8,2,4096]{3,2,1,0:T(2,128)(2,1)} %copy.102) | data formatting | bytes 8388608 | tf_op jit(solution)/shard_map/reshape | solution.py:95
  304.5 294.0 %while.13 = (s32[]{:T(128)}, bf16[8,64,64,64]{3,2,1,0:T(8,128)(2,1)}, f32[8,8,1024]{2,1,0:T(8,128)S(1)}, s32[8,64,3]{1,0,2:T(8,128)S(1)}, bf16[8,8,64,1024]{3,2,...) while((s32[]{:T(128)}, ...), condition=%wide.region_6.7_spmd.clone, body=%wide.region_4.6_spmd.clone.sunk | while | flops 1105398272 | bytes 70560616 | solution.py:118
  304.7 8.9 %gather_fusion = bf16[64,64,1024]{2,1,0:T(8,128)(2,1)} fusion(bf16[8,8,64,1024]{3,2,1,0:T(8,128)(2,1)} %get-tuple-element.215, s32[64]{0:T(128)S(1)} %get-tuple-element.191), kind=kCustom, calls=%fused_computation.2.clone.clone.1 | custom fusion | bytes 16777728 | tf_op jit(solution)/shard_map/while/body/eval_jaxpr/gather | solution.py:103
  313.6 8.9 %gather_fusion.1 = bf16[64,64,1024]{2,1,0:T(8,128)(2,1)} fusion(bf16[8,8,64,1024]{3,2,1,0:T(8,128)(2,1)} %get-tuple-element.215, s32[64]{0:T(128)S(1)} %get-tuple-element.192), kind=kCustom, calls=%fused_computation.clone.clone.1 | custom fusion | bytes 16777728 | tf_op jit(solution)/shard_map/while/body/eval_jaxpr/gather | solution.py:102
  323.3 9.2 %fusion.167 = bf16[8,64,64,64]{3,2,1,0:T(8,128)(2,1)} fusion(bf16[8,64,64,64]{3,2,1,0:T(8,128)(2,1)} %get-tuple-element.204, s32[]{:T(128)S(6)} %copy.132, bf16[64,64,1024]{2,1,0:T(8,128)(2,1)} %gather_fusion, bf16[64,64,1024]{2,1,0:T(8,128)(2,1)} %gather_fusion.1, f32[64,1024]{1,0:T(8,128)S(1)} %gather_fusion.2), kind=kOutput, calls=%fused_computation.15.clone.1 | convolution fusion | flops 549715968 | bytes 18087940 | tf_op jit(solution)/shard_map/while/body/eval_jaxpr/sig,sjg->sij/dot_general | solution.py:111
  332.4 8.7 %fusion.168 = f32[64,1024]{1,0:T(8,128)S(1)} fusion(bf16[64,64,1024]{2,1,0:T(8,128)(2,1)} %gather_fusion.1, bf16[64,64,1024]{2,1,0:T(8,128)(2,1)} %gather_fusion, bf16[8,64,64,64]{3,2,1,0:T(8,128)(2,1)} %get-tuple-element.217, s32[]{:T(128)S(6)} %copy.132), kind=kOutput, calls=%fused_computation.10.clone.1 | convolution fusion | flops 549388288 | bytes 18087940 | tf_op jit(solution)/shard_map/while/body/eval_jaxpr/sij,sjg->sig/dot_general | solution.py:104
  341.5 8.9 %gather_fusion = bf16[64,64,1024]{2,1,0:T(8,128)(2,1)} fusion(bf16[8,8,64,1024]{3,2,1,0:T(8,128)(2,1)} %get-tuple-element.215, s32[64]{0:T(128)S(1)} %get-tuple-element.191), kind=kCustom, calls=%fused_computation.2.clone.clone.1 | custom fusion | bytes 16777728 | tf_op jit(solution)/shard_map/while/body/eval_jaxpr/gather | solution.py:103
  350.4 8.9 %gather_fusion.1 = bf16[64,64,1024]{2,1,0:T(8,128)(2,1)} fusion(bf16[8,8,64,1024]{3,2,1,0:T(8,128)(2,1)} %get-tuple-element.215, s32[64]{0:T(128)S(1)} %get-tuple-element.192), kind=kCustom, calls=%fused_computation.clone.clone.1 | custom fusion | bytes 16777728 | tf_op jit(solution)/shard_map/while/body/eval_jaxpr/gather | solution.py:102
  360.0 9.1 %fusion.167 = bf16[8,64,64,64]{3,2,1,0:T(8,128)(2,1)} fusion(bf16[8,64,64,64]{3,2,1,0:T(8,128)(2,1)} %get-tuple-element.204, s32[]{:T(128)S(6)} %copy.132, bf16[64,64,1024]{2,1,0:T(8,128)(2,1)} %gather_fusion, bf16[64,64,1024]{2,1,0:T(8,128)(2,1)} %gather_fusion.1, f32[64,1024]{1,0:T(8,128)S(1)} %gather_fusion.2), kind=kOutput, calls=%fused_computation.15.clone.1 | convolution fusion | flops 549715968 | bytes 18087940 | tf_op jit(solution)/shard_map/while/body/eval_jaxpr/sig,sjg->sij/dot_general | solution.py:111
  369.1 8.7 %fusion.168 = f32[64,1024]{1,0:T(8,128)S(1)} fusion(bf16[64,64,1024]{2,1,0:T(8,128)(2,1)} %gather_fusion.1, bf16[64,64,1024]{2,1,0:T(8,128)(2,1)} %gather_fusion, bf16[8,64,64,64]{3,2,1,0:T(8,128)(2,1)} %get-tuple-element.217, s32[]{:T(128)S(6)} %copy.132), kind=kOutput, calls=%fused_computation.10.clone.1 | convolution fusion | flops 549388288 | bytes 18087940 | tf_op jit(solution)/shard_map/while/body/eval_jaxpr/sij,sjg->sig/dot_general | solution.py:104
  378.2 8.9 %gather_fusion = bf16[64,64,1024]{2,1,0:T(8,128)(2,1)} fusion(bf16[8,8,64,1024]{3,2,1,0:T(8,128)(2,1)} %get-tuple-element.215, s32[64]{0:T(128)S(1)} %get-tuple-element.191), kind=kCustom, calls=%fused_computation.2.clone.clone.1 | custom fusion | bytes 16777728 | tf_op jit(solution)/shard_map/while/body/eval_jaxpr/gather | solution.py:103
  387.1 8.9 %gather_fusion.1 = bf16[64,64,1024]{2,1,0:T(8,128)(2,1)} fusion(bf16[8,8,64,1024]{3,2,1,0:T(8,128)(2,1)} %get-tuple-element.215, s32[64]{0:T(128)S(1)} %get-tuple-element.192), kind=kCustom, calls=%fused_computation.clone.clone.1 | custom fusion | bytes 16777728 | tf_op jit(solution)/shard_map/while/body/eval_jaxpr/gather | solution.py:102
  396.7 9.1 %fusion.167 = bf16[8,64,64,64]{3,2,1,0:T(8,128)(2,1)} fusion(bf16[8,64,64,64]{3,2,1,0:T(8,128)(2,1)} %get-tuple-element.204, s32[]{:T(128)S(6)} %copy.132, bf16[64,64,1024]{2,1,0:T(8,128)(2,1)} %gather_fusion, bf16[64,64,1024]{2,1,0:T(8,128)(2,1)} %gather_fusion.1, f32[64,1024]{1,0:T(8,128)S(1)} %gather_fusion.2), kind=kOutput, calls=%fused_computation.15.clone.1 | convolution fusion | flops 549715968 | bytes 18087940 | tf_op jit(solution)/shard_map/while/body/eval_jaxpr/sig,sjg->sij/dot_general | solution.py:111
  405.8 8.7 %fusion.168 = f32[64,1024]{1,0:T(8,128)S(1)} fusion(bf16[64,64,1024]{2,1,0:T(8,128)(2,1)} %gather_fusion.1, bf16[64,64,1024]{2,1,0:T(8,128)(2,1)} %gather_fusion, bf16[8,64,64,64]{3,2,1,0:T(8,128)(2,1)} %get-tuple-element.217, s32[]{:T(128)S(6)} %copy.132), kind=kOutput, calls=%fused_computation.10.clone.1 | convolution fusion | flops 549388288 | bytes 18087940 | tf_op jit(solution)/shard_map/while/body/eval_jaxpr/sij,sjg->sig/dot_general | solution.py:104
  414.9 8.9 %gather_fusion = bf16[64,64,1024]{2,1,0:T(8,128)(2,1)} fusion(bf16[8,8,64,1024]{3,2,1,0:T(8,128)(2,1)} %get-tuple-element.215, s32[64]{0:T(128)S(1)} %get-tuple-element.191), kind=kCustom, calls=%fused_computation.2.clone.clone.1 | custom fusion | bytes 16777728 | tf_op jit(solution)/shard_map/while/body/eval_jaxpr/gather | solution.py:103
  423.7 8.9 %gather_fusion.1 = bf16[64,64,1024]{2,1,0:T(8,128)(2,1)} fusion(bf16[8,8,64,1024]{3,2,1,0:T(8,128)(2,1)} %get-tuple-element.215, s32[64]{0:T(128)S(1)} %get-tuple-element.192), kind=kCustom, calls=%fused_computation.clone.clone.1 | custom fusion | bytes 16777728 | tf_op jit(solution)/shard_map/while/body/eval_jaxpr/gather | solution.py:102
  433.3 9.1 %fusion.167 = bf16[8,64,64,64]{3,2,1,0:T(8,128)(2,1)} fusion(bf16[8,64,64,64]{3,2,1,0:T(8,128)(2,1)} %get-tuple-element.204, s32[]{:T(128)S(6)} %copy.132, bf16[64,64,1024]{2,1,0:T(8,128)(2,1)} %gather_fusion, bf16[64,64,1024]{2,1,0:T(8,128)(2,1)} %gather_fusion.1, f32[64,1024]{1,0:T(8,128)S(1)} %gather_fusion.2), kind=kOutput, calls=%fused_computation.15.clone.1 | convolution fusion | flops 549715968 | bytes 18087940 | tf_op jit(solution)/shard_map/while/body/eval_jaxpr/sig,sjg->sij/dot_general | solution.py:111
  442.4 8.7 %fusion.168 = f32[64,1024]{1,0:T(8,128)S(1)} fusion(bf16[64,64,1024]{2,1,0:T(8,128)(2,1)} %gather_fusion.1, bf16[64,64,1024]{2,1,0:T(8,128)(2,1)} %gather_fusion, bf16[8,64,64,64]{3,2,1,0:T(8,128)(2,1)} %get-tuple-element.217, s32[]{:T(128)S(6)} %copy.132), kind=kOutput, calls=%fused_computation.10.clone.1 | convolution fusion | flops 549388288 | bytes 18087940 | tf_op jit(solution)/shard_map/while/body/eval_jaxpr/sij,sjg->sig/dot_general | solution.py:104
  451.4 9.0 %gather_fusion = bf16[64,64,1024]{2,1,0:T(8,128)(2,1)} fusion(bf16[8,8,64,1024]{3,2,1,0:T(8,128)(2,1)} %get-tuple-element.215, s32[64]{0:T(128)S(1)} %get-tuple-element.191), kind=kCustom, calls=%fused_computation.2.clone.clone.1 | custom fusion | bytes 16777728 | tf_op jit(solution)/shard_map/while/body/eval_jaxpr/gather | solution.py:103
  460.4 8.9 %gather_fusion.1 = bf16[64,64,1024]{2,1,0:T(8,128)(2,1)} fusion(bf16[8,8,64,1024]{3,2,1,0:T(8,128)(2,1)} %get-tuple-element.215, s32[64]{0:T(128)S(1)} %get-tuple-element.192), kind=kCustom, calls=%fused_computation.clone.clone.1 | custom fusion | bytes 16777728 | tf_op jit(solution)/shard_map/while/body/eval_jaxpr/gather | solution.py:102
  470.0 9.2 %fusion.167 = bf16[8,64,64,64]{3,2,1,0:T(8,128)(2,1)} fusion(bf16[8,64,64,64]{3,2,1,0:T(8,128)(2,1)} %get-tuple-element.204, s32[]{:T(128)S(6)} %copy.132, bf16[64,64,1024]{2,1,0:T(8,128)(2,1)} %gather_fusion, bf16[64,64,1024]{2,1,0:T(8,128)(2,1)} %gather_fusion.1, f32[64,1024]{1,0:T(8,128)S(1)} %gather_fusion.2), kind=kOutput, calls=%fused_computation.15.clone.1 | convolution fusion | flops 549715968 | bytes 18087940 | tf_op jit(solution)/shard_map/while/body/eval_jaxpr/sig,sjg->sij/dot_general | solution.py:111
  479.2 8.7 %fusion.168 = f32[64,1024]{1,0:T(8,128)S(1)} fusion(bf16[64,64,1024]{2,1,0:T(8,128)(2,1)} %gather_fusion.1, bf16[64,64,1024]{2,1,0:T(8,128)(2,1)} %gather_fusion, bf16[8,64,64,64]{3,2,1,0:T(8,128)(2,1)} %get-tuple-element.217, s32[]{:T(128)S(6)} %copy.132), kind=kOutput, calls=%fused_computation.10.clone.1 | convolution fusion | flops 549388288 | bytes 18087940 | tf_op jit(solution)/shard_map/while/body/eval_jaxpr/sij,sjg->sig/dot_general | solution.py:104
  488.3 9.0 %gather_fusion = bf16[64,64,1024]{2,1,0:T(8,128)(2,1)} fusion(bf16[8,8,64,1024]{3,2,1,0:T(8,128)(2,1)} %get-tuple-element.215, s32[64]{0:T(128)S(1)} %get-tuple-element.191), kind=kCustom, calls=%fused_computation.2.clone.clone.1 | custom fusion | bytes 16777728 | tf_op jit(solution)/shard_map/while/body/eval_jaxpr/gather | solution.py:103
  497.2 9.0 %gather_fusion.1 = bf16[64,64,1024]{2,1,0:T(8,128)(2,1)} fusion(bf16[8,8,64,1024]{3,2,1,0:T(8,128)(2,1)} %get-tuple-element.215, s32[64]{0:T(128)S(1)} %get-tuple-element.192), kind=kCustom, calls=%fused_computation.clone.clone.1 | custom fusion | bytes 16777728 | tf_op jit(solution)/shard_map/while/body/eval_jaxpr/gather | solution.py:102
  506.9 9.1 %fusion.167 = bf16[8,64,64,64]{3,2,1,0:T(8,128)(2,1)} fusion(bf16[8,64,64,64]{3,2,1,0:T(8,128)(2,1)} %get-tuple-element.204, s32[]{:T(128)S(6)} %copy.132, bf16[64,64,1024]{2,1,0:T(8,128)(2,1)} %gather_fusion, bf16[64,64,1024]{2,1,0:T(8,128)(2,1)} %gather_fusion.1, f32[64,1024]{1,0:T(8,128)S(1)} %gather_fusion.2), kind=kOutput, calls=%fused_computation.15.clone.1 | convolution fusion | flops 549715968 | bytes 18087940 | tf_op jit(solution)/shard_map/while/body/eval_jaxpr/sig,sjg->sij/dot_general | solution.py:111
  516.0 8.7 %fusion.168 = f32[64,1024]{1,0:T(8,128)S(1)} fusion(bf16[64,64,1024]{2,1,0:T(8,128)(2,1)} %gather_fusion.1, bf16[64,64,1024]{2,1,0:T(8,128)(2,1)} %gather_fusion, bf16[8,64,64,64]{3,2,1,0:T(8,128)(2,1)} %get-tuple-element.217, s32[]{:T(128)S(6)} %copy.132), kind=kOutput, calls=%fused_computation.10.clone.1 | convolution fusion | flops 549388288 | bytes 18087940 | tf_op jit(solution)/shard_map/while/body/eval_jaxpr/sij,sjg->sig/dot_general | solution.py:104
  525.0 8.9 %gather_fusion = bf16[64,64,1024]{2,1,0:T(8,128)(2,1)} fusion(bf16[8,8,64,1024]{3,2,1,0:T(8,128)(2,1)} %get-tuple-element.215, s32[64]{0:T(128)S(1)} %get-tuple-element.191), kind=kCustom, calls=%fused_computation.2.clone.clone.1 | custom fusion | bytes 16777728 | tf_op jit(solution)/shard_map/while/body/eval_jaxpr/gather | solution.py:103
  534.0 8.9 %gather_fusion.1 = bf16[64,64,1024]{2,1,0:T(8,128)(2,1)} fusion(bf16[8,8,64,1024]{3,2,1,0:T(8,128)(2,1)} %get-tuple-element.215, s32[64]{0:T(128)S(1)} %get-tuple-element.192), kind=kCustom, calls=%fused_computation.clone.clone.1 | custom fusion | bytes 16777728 | tf_op jit(solution)/shard_map/while/body/eval_jaxpr/gather | solution.py:102
  543.6 9.1 %fusion.167 = bf16[8,64,64,64]{3,2,1,0:T(8,128)(2,1)} fusion(bf16[8,64,64,64]{3,2,1,0:T(8,128)(2,1)} %get-tuple-element.204, s32[]{:T(128)S(6)} %copy.132, bf16[64,64,1024]{2,1,0:T(8,128)(2,1)} %gather_fusion, bf16[64,64,1024]{2,1,0:T(8,128)(2,1)} %gather_fusion.1, f32[64,1024]{1,0:T(8,128)S(1)} %gather_fusion.2), kind=kOutput, calls=%fused_computation.15.clone.1 | convolution fusion | flops 549715968 | bytes 18087940 | tf_op jit(solution)/shard_map/while/body/eval_jaxpr/sig,sjg->sij/dot_general | solution.py:111
  552.7 8.7 %fusion.168 = f32[64,1024]{1,0:T(8,128)S(1)} fusion(bf16[64,64,1024]{2,1,0:T(8,128)(2,1)} %gather_fusion.1, bf16[64,64,1024]{2,1,0:T(8,128)(2,1)} %gather_fusion, bf16[8,64,64,64]{3,2,1,0:T(8,128)(2,1)} %get-tuple-element.217, s32[]{:T(128)S(6)} %copy.132), kind=kOutput, calls=%fused_computation.10.clone.1 | convolution fusion | flops 549388288 | bytes 18087940 | tf_op jit(solution)/shard_map/while/body/eval_jaxpr/sij,sjg->sig/dot_general | solution.py:104
  561.8 8.9 %gather_fusion = bf16[64,64,1024]{2,1,0:T(8,128)(2,1)} fusion(bf16[8,8,64,1024]{3,2,1,0:T(8,128)(2,1)} %get-tuple-element.215, s32[64]{0:T(128)S(1)} %get-tuple-element.191), kind=kCustom, calls=%fused_computation.2.clone.clone.1 | custom fusion | bytes 16777728 | tf_op jit(solution)/shard_map/while/body/eval_jaxpr/gather | solution.py:103
  570.7 8.9 %gather_fusion.1 = bf16[64,64,1024]{2,1,0:T(8,128)(2,1)} fusion(bf16[8,8,64,1024]{3,2,1,0:T(8,128)(2,1)} %get-tuple-element.215, s32[64]{0:T(128)S(1)} %get-tuple-element.192), kind=kCustom, calls=%fused_computation.clone.clone.1 | custom fusion | bytes 16777728 | tf_op jit(solution)/shard_map/while/body/eval_jaxpr/gather | solution.py:102
  580.3 9.1 %fusion.167 = bf16[8,64,64,64]{3,2,1,0:T(8,128)(2,1)} fusion(bf16[8,64,64,64]{3,2,1,0:T(8,128)(2,1)} %get-tuple-element.204, s32[]{:T(128)S(6)} %copy.132, bf16[64,64,1024]{2,1,0:T(8,128)(2,1)} %gather_fusion, bf16[64,64,1024]{2,1,0:T(8,128)(2,1)} %gather_fusion.1, f32[64,1024]{1,0:T(8,128)S(1)} %gather_fusion.2), kind=kOutput, calls=%fused_computation.15.clone.1 | convolution fusion | flops 549715968 | bytes 18087940 | tf_op jit(solution)/shard_map/while/body/eval_jaxpr/sig,sjg->sij/dot_general | solution.py:111
  589.4 8.7 %fusion.168 = f32[64,1024]{1,0:T(8,128)S(1)} fusion(bf16[64,64,1024]{2,1,0:T(8,128)(2,1)} %gather_fusion.1, bf16[64,64,1024]{2,1,0:T(8,128)(2,1)} %gather_fusion, bf16[8,64,64,64]{3,2,1,0:T(8,128)(2,1)} %get-tuple-element.217, s32[]{:T(128)S(6)} %copy.132), kind=kOutput, calls=%fused_computation.10.clone.1 | convolution fusion | flops 549388288 | bytes 18087940 | tf_op jit(solution)/shard_map/while/body/eval_jaxpr/sij,sjg->sig/dot_general | solution.py:104
  598.5 14.0 %reshape.83 = bf16[32,8,2,4096]{3,2,1,0:T(2,128)(2,1)} reshape(bf16[8,64,64,64]{3,2,1,0:T(8,128)(2,1)} %get-tuple-element.47) | data formatting | bytes 8388608 | tf_op jit(solution)/shard_map/reshape | solution.py:120
  612.5 64.1 %all_to_all.40 = bf16[32,8,2,4096]{3,2,1,0:T(2,128)(2,1)S(1)} all-to-all(bf16[32,8,2,4096]{3,2,1,0:T(2,128)(2,1)} %reshape.83), channel_id=1, replica_groups=mesh['row'=32,'col'=8] {'row'}, dimensions={0} | all-to-all | bytes 8388608 | tf_op jit(solution)/shard_map/all_to_all | solution.py:122
  676.6 6.1 copy.104
  682.7 51.4 %all-to-all-start.6 = ((bf16[32,8,2,4096]{3,2,0,1:T(2,128)(2,1)}), bf16[32,8,2,4096]{3,2,0,1:T(2,128)(2,1)}, u32[]{:S(2)}, u32[]{:S(2)}) async-start(bf16[32,8,2,4096]{3,2,0,1:T(2,128)(2,1)} %copy.104), calls=%async_computation.6 | async-start | bytes 8388608 | tf_op jit(solution)/shard_map/all_to_all | solution.py:121
  738.8 87.5 %collective-permute-done = bf16[2,5,64,64]{2,3,1,0:T(8,128)(2,1)S(1)} collective-permute-done((bf16[2,5,64,64]{2,3,1,0:T(8,128)(2,1)S(1)}, bf16[2,5,64,64]{2,3,1,0:T(8,128)(2,1)S(1)}, u32[]{:S(2)}, u32[]{:S(2)}) %collective-permute-start) | collective-permute-done | bytes 81952 | tf_op jit(solution)/shard_map/ppermute | solution.py:16
  841.8 10.1 %copy.105 = bf16[32,8,2,4096]{3,2,1,0:T(2,128)(2,1)} copy(bf16[32,8,2,4096]{3,2,0,1:T(2,128)(2,1)} %all-to-all-done.6) | data formatting | bytes 8388608 | tf_op jit(solution)/shard_map/all_to_all | solution.py:121
  851.9 7.2 reshape.84
  (110 shorter events, 67.7 us)
Async XLA Ops:
  30.7 21.4 %all-to-all-start.1 = ((bf16[32,8,2,3]{0,2,3,1:T(2,128)(2,1)}), bf16[32,8,2,3]{0,2,3,1:T(2,128)(2,1)S(1)}, u32[]{:S(2)}, u32[]{:S(2)}) async-start(bf16[32,8,2,3]{0,2,3,1:T(2,128)(2,1)} %copy.97), calls=%async_computation.1 | async-start | bytes 24576 | tf_op jit(solution)/shard_map/all_to_all | solution.py:85
  52.1 5.0 copy-start.1
  52.1 105.8 %all-to-all-start.3 = ((bf16[32,8,2,4096]{3,2,1,0:T(2,128)(2,1)}), bf16[32,8,2,4096]{3,2,1,0:T(2,128)(2,1)}, u32[]{:S(2)}, u32[]{:S(2)}) async-start(bf16[32,8,2,4096]{3,2,1,0:T(2,128)(2,1)} %reshape.80), calls=%async_computation.3 | async-start | bytes 8388608 | tf_op jit(solution)/shard_map/all_to_all | solution.py:79
  157.9 15.1 %all-to-all-start.2 = ((f32[1,32,256]{2,0,1:T(1,128)}), f32[1,32,256]{2,0,1:T(1,128)S(1)}, u32[]{:S(2)}, u32[]{:S(2)}) async-start(f32[1,32,256]{2,0,1:T(1,128)} %copy.100), calls=%async_computation.2 | async-start | bytes 65536 | tf_op jit(solution)/shard_map/all_to_all | solution.py:45
  172.9 107.3 %all-to-all-start.4 = ((bf16[32,8,2,4096]{3,2,0,1:T(2,128)(2,1)}), bf16[32,8,2,4096]{3,2,0,1:T(2,128)(2,1)}, u32[]{:S(2)}, u32[]{:S(2)}) async-start(bf16[32,8,2,4096]{3,2,0,1:T(2,128)(2,1)} %copy.101), calls=%async_computation.4 | async-start | bytes 8388608 | tf_op jit(solution)/shard_map/all_to_all | solution.py:78
  682.7 159.1 %all-to-all-start.6 = ((bf16[32,8,2,4096]{3,2,0,1:T(2,128)(2,1)}), bf16[32,8,2,4096]{3,2,0,1:T(2,128)(2,1)}, u32[]{:S(2)}, u32[]{:S(2)}) async-start(bf16[32,8,2,4096]{3,2,0,1:T(2,128)(2,1)} %copy.104), calls=%async_computation.6 | async-start | bytes 8388608 | tf_op jit(solution)/shard_map/all_to_all | solution.py:121
  737.0 91.1 %collective-permute-start.1 = (bf16[2,5,64,64]{2,3,1,0:T(8,128)(2,1)S(1)}, bf16[2,5,64,64]{2,3,1,0:T(8,128)(2,1)S(1)}, u32[]{:S(2)}, u32[]{:S(2)}) collective-permute-start(bf16[2,5,64,64]{2,3,1,0:T(8,128)(2,1)S(1)} %get-tuple-element.140), channel_id=1, source_target_pairs={{1,0},{2,1},{3,2},{4,3},{5,4},{6,5},{7,6},{8,7},{9,8},{10,9},{11,1... | collective-permute-start | bytes 245768 | tf_op jit(solution)/shard_map/ppermute | solution.py:17
  737.5 88.8 %collective-permute-start = (bf16[2,5,64,64]{2,3,1,0:T(8,128)(2,1)S(1)}, bf16[2,5,64,64]{2,3,1,0:T(8,128)(2,1)S(1)}, u32[]{:S(2)}, u32[]{:S(2)}) collective-permute-start(bf16[2,5,64,64]{2,3,1,0:T(8,128)(2,1)S(1)} %get-tuple-element.141), channel_id=1, source_target_pairs={{0,1},{1,2},{2,3},{3,4},{4,5},{5,6},{6,7},{7,8},{8,9},{9,10},{10,1... | collective-permute-start | bytes 245768 | tf_op jit(solution)/shard_map/ppermute | solution.py:16
  828.5 1.5 copy-start
where the time goes:
time: 876 us; the launch traced here: 867 us
  waiting for transfers between devices  280 us (32%)
  local copies, waits for them, and re-layouts  259 us (30%)
  matrix products  152 us (17%)
  blocking collectives  87.7 us (10%)
  starting transfers between devices  85 us (10%)
    all_to_all x1, waiting for transfers between devices, local(): lax.all_to_all(outgoing, 'row', split_axis=0, concat_axis=0, tiled=True)  100 us
    all_to_all x1, waiting for transfers between devices, local(): lax.all_to_all(lax.all_to_all(outgoing, 'row', split_axis=0, concat_axis=...  89.9 us
    ppermute x1, waiting for transfers between devices, padded(): before = lax.ppermute(last, axis, up)  87.5 us
    dot_general x8, matrix products, handle(): jnp.einsum('sig,sjg->sij', scaled, second_basis, preferred_element_type=j...  72.9 us
    gather x8, local copies, waits for them, and re-layouts, handle(): second_basis = basis_values[task_ids, tags[:, 2]]  71.5 us
    gather x8, local copies, waits for them, and re-layouts, handle(): first_basis = basis_values[task_ids, tags[:, 1]]  71.4 us
    dot_general x8, matrix products, handle(): jnp.einsum('sij,sjg->sig', blocks, second_basis, preferred_element_type=j...  69.8 us
    all_to_all x1, blocking collectives, local(): lax.all_to_all(results, 'row', split_axis=0, concat_axis=0, tiled=True)  64.1 us
  transfers between devices with their start and end apart: 7, of which 5 were waited for; matrix products, arithmetic and copies ran while one was open for 5% of the time, Pallas kernels for 0%

commit v1 on v0

v1 whole, which is shorter than its diff:
```python
import functools

import jax
import jax.numpy as jnp
from jax import lax
from jax.experimental import pallas as pl
from jax.experimental.pallas import tpu as pltpu
from jax.sharding import PartitionSpec as P

HALF = 2
PAIRS = 120
PEERS = 256
SLOTS_ALL = 512
ROWS = 32
LANES = 128
BF = 64
TASKS = 8
BASIS = 512
POINTS = 1024
ALL = ("row", "col")
VMEM_LIMIT = 56 * 1024 * 1024


def padded(array, sides, width):
    for axis, dim in sides:
        size, length = (lax.axis_size(axis), array.shape[dim])
        up = [(i, (i + 1) % size) for i in range(size)]
        down = [(j, i) for i, j in up]
        last = lax.slice_in_dim(array, length - width, length, axis=dim)
        first = lax.slice_in_dim(array, 0, width, axis=dim)
        before = lax.ppermute(last, axis, up)
        after = lax.ppermute(first, axis, down)
        array = jnp.concatenate([before, array, after], axis=dim)
    return array


def margin_of(density, margin):
    atoms_here = density.shape[0]
    offsets = density.shape[1]
    extended = padded(margin, ((ALL, 0),), HALF)
    columns = []
    for offset in range(offsets):
        lowest = max(0, offset - HALF)
        highest = min(offsets - 1, offset + HALF)
        left_blocks = density[:, lowest : highest + 1]
        right_blocks = jnp.stack(
            [extended[middle : middle + atoms_here, offset - middle + HALF] for middle in range(lowest, highest + 1)],
            axis=1,
        )
        columns.append(jnp.einsum("amik,amkj->aij", left_blocks, right_blocks, preferred_element_type=jnp.float32))
    return jnp.stack(columns, axis=1).astype(jnp.bfloat16)


def pack_kernel(place, density, out):
    def body(step, carry):
        for inner in range(8):
            pair = step * 8 + inner
            block = density[pair]
            spot = place[pair]
            out[spot, :, 0:BF] = block[0:ROWS]
            out[spot, :, BF:LANES] = block[ROWS:BF]
        return carry

    lax.fori_loop(0, PAIRS // 8, body, 0)


def unpack_kernel(place, blocks, out):
    def body(step, carry):
        for inner in range(8):
            pair = step * 8 + inner
            block = blocks[place[pair]]
            out[pair, 0:ROWS] = block[:, 0:BF]
            out[pair, ROWS:BF] = block[:, BF:LANES]
        return carry

    lax.fori_loop(0, PAIRS // 8, body, 0)


def matrix_kernel(label, basis, potential, out, scaled, table):
    task = pl.program_id(0)
    phi = basis[0]
    scaled[...] = (phi.astype(jnp.float32) * potential[0]).astype(jnp.bfloat16)
    full = lax.dot_general(
        scaled[...], phi, (((1,), (1,)), ((), ())), preferred_element_type=jnp.float32
    )
    left = lax.broadcasted_iota(jnp.int32, (ROWS, LANES), 1) < BF
    for first in range(8):
        for pair in range(4):
            columns = slice(pair * LANES, (pair + 1) * LANES)
            top = full[first * BF : first * BF + ROWS, columns]
            low = full[first * BF + ROWS : (first + 1) * BF, columns]
            spot = task * 64 + first * 8 + 2 * pair
            table[spot] = jnp.where(left, top, pltpu.roll(low, BF, 1)).astype(jnp.bfloat16)
            table[spot + 1] = jnp.where(left, pltpu.roll(top, BF, 1), low).astype(jnp.bfloat16)

    @pl.when(task == TASKS - 1)
    def _():
        def body(step, carry):
            for inner in range(16):
                slot = step * 16 + inner
                out[slot] = table[jnp.maximum(label[slot], 0)]
            return carry

        lax.fori_loop(0, SLOTS_ALL // 16, body, 0)


def grid_kernel(label, blocks, basis, out, table, weights):
    task = pl.program_id(0)

    @pl.when(task == 0)
    def _():
        def clear(step, carry):
            for inner in range(8):
                table[step * 8 + inner] = jnp.zeros((ROWS, LANES), jnp.float32)
            return carry

        lax.fori_loop(0, SLOTS_ALL // 8, clear, 0)

        def body(step, carry):
            for inner in range(8):
                slot = step * 8 + inner
                which = label[slot]
                spot = jnp.where(which < 0, SLOTS_ALL, which)
                table[spot] = table[spot] + blocks[slot].astype(jnp.float32)
            return carry

        lax.fori_loop(0, SLOTS_ALL // 8, body, 0)

    left = lax.broadcasted_iota(jnp.int32, (ROWS, LANES), 1) < BF
    for first in range(8):
        for pair in range(4):
            spot = task * 64 + first * 8 + 2 * pair
            one = table[spot]
            two = table[spot + 1]
            columns = slice(pair * LANES, (pair + 1) * LANES)
            weights[first * BF : first * BF + ROWS, columns] = jnp.where(left, one, pltpu.roll(two, BF, 1)).astype(
                jnp.bfloat16
            )
            weights[first * BF + ROWS : (first + 1) * BF, columns] = jnp.where(left, pltpu.roll(one, BF, 1), two).astype(
                jnp.bfloat16
            )
    for piece in range(4):
        columns = slice(piece * 256, (piece + 1) * 256)
        phi = basis[0, :, columns]
        weighted = jnp.dot(weights[...], phi, preferred_element_type=jnp.float32)
        out[0, :, columns] = jnp.sum(phi.astype(jnp.float32) * weighted, axis=0, keepdims=True)


def params(**more):
    return pltpu.CompilerParams(vmem_limit_bytes=VMEM_LIMIT, **more)


SMEM = pl.BlockSpec(memory_space=pltpu.SMEM)
BLOCKS = jax.ShapeDtypeStruct((SLOTS_ALL, ROWS, LANES), jnp.bfloat16)


def whole(shape):
    return pl.BlockSpec(shape, lambda *_: (0,) * len(shape))


def local(density, margin, potential, basis_values, pair_owner, pair_box, pair_slots):
    atoms_here, offsets = density.shape[:2]
    owners = pair_owner.reshape(PAIRS)
    same = owners[:, None] == owners[None, :]
    before = jnp.arange(PAIRS)[:, None] > jnp.arange(PAIRS)[None, :]
    ranks = jnp.sum((same & before).astype(jnp.int32), axis=1)
    places = owners * 2 + ranks
    fields = jnp.stack(
        [pair_box.reshape(PAIRS), pair_slots[..., 0].reshape(PAIRS), pair_slots[..., 1].reshape(PAIRS)], axis=0
    )
    chosen = jnp.arange(SLOTS_ALL, dtype=jnp.int32)[None, :, None] == places[None, None, :]
    sent = jnp.sum(jnp.where(chosen, fields[:, None, :] + 1, 0), axis=2) - 1
    sent = sent.reshape(3, PEERS, 2).transpose(1, 0, 2).reshape(PEERS, 1, 6)
    sent = jnp.pad(sent, ((0, 0), (0, 0), (0, LANES - 6)))
    tags = lax.all_to_all(sent, ALL, 0, 0, tiled=True).reshape(PEERS, LANES)[:, :6].reshape(PEERS, 3, 2)
    labels = jnp.where(tags[:, 0] < 0, -1, tags[:, 0] * 64 + tags[:, 1] * 8 + tags[:, 2]).reshape(SLOTS_ALL)

    flat = density.reshape(PAIRS, BF, BF)
    outgoing = pl.pallas_call(
        pack_kernel,
        out_shape=BLOCKS,
        in_specs=[SMEM, pl.BlockSpec(memory_space=pltpu.VMEM)],
        out_specs=pl.BlockSpec(memory_space=pltpu.VMEM),
        compiler_params=params(),
        cost_estimate=pl.CostEstimate(flops=0, bytes_accessed=6 << 20, transcendentals=0),
        name="pack",
    )(places, flat)
    arrived = lax.all_to_all(outgoing.reshape(PEERS, 64, LANES), ALL, 0, 0, tiled=True).reshape(BLOCKS.shape)

    pencil = lax.all_to_all(potential, "row", split_axis=1, concat_axis=0, tiled=True)
    box_potential = pencil.reshape(TASKS, 1, POINTS)
    phi = basis_values.reshape(TASKS, BASIS, POINTS)

    results = pl.pallas_call(
        matrix_kernel,
        out_shape=BLOCKS,
        grid=(TASKS,),
        in_specs=[
            SMEM,
            pl.BlockSpec((1, BASIS, POINTS), lambda t: (t, 0, 0)),
            pl.BlockSpec((1, 1, POINTS), lambda t: (t, 0, 0)),
        ],
        out_specs=whole(BLOCKS.shape),
        scratch_shapes=[
            pltpu.VMEM((BASIS, POINTS), jnp.bfloat16),
            pltpu.VMEM((SLOTS_ALL, ROWS, LANES), jnp.bfloat16),
        ],
        compiler_params=params(),
        cost_estimate=pl.CostEstimate(flops=2 * TASKS * BASIS * BASIS * POINTS, bytes_accessed=14 << 20, transcendentals=0),
        name="matrices",
    )(labels, phi, box_potential)
    returned = lax.all_to_all(results.reshape(PEERS, 64, LANES), ALL, 0, 0, tiled=True).reshape(BLOCKS.shape)

    grid_rows = pl.pallas_call(
        grid_kernel,
        out_shape=jax.ShapeDtypeStruct((TASKS, 1, POINTS), jnp.float32),
        grid=(TASKS,),
        in_specs=[SMEM, whole(BLOCKS.shape), pl.BlockSpec((1, BASIS, POINTS), lambda t: (t, 0, 0))],
        out_specs=pl.BlockSpec((1, 1, POINTS), lambda t: (t, 0, 0)),
        scratch_shapes=[
            pltpu.VMEM((SLOTS_ALL + 1, ROWS, LANES), jnp.float32),
            pltpu.VMEM((BASIS, BASIS), jnp.bfloat16),
        ],
        compiler_params=params(),
        cost_estimate=pl.CostEstimate(flops=2 * TASKS * BASIS * BASIS * POINTS, bytes_accessed=14 << 20, transcendentals=0),
        name="collocate",
    )(labels, arrived, phi)
    density_grid = grid_rows.reshape(pencil.shape)

    ks_blocks = pl.pallas_call(
        unpack_kernel,
        out_shape=jax.ShapeDtypeStruct((PAIRS, BF, BF), jnp.bfloat16),
        in_specs=[SMEM, pl.BlockSpec(memory_space=pltpu.VMEM)],
        out_specs=pl.BlockSpec(memory_space=pltpu.VMEM),
        compiler_params=params(),
        cost_estimate=pl.CostEstimate(flops=0, bytes_accessed=6 << 20, transcendentals=0),
        name="unpack",
    )(places, returned).reshape(atoms_here, offsets, BF, BF)
    return density_grid, ks_blocks, margin_of(density, margin)


def solution(mesh):
    placed = (
        P(ALL, None, None, None),
        P(ALL, None, None, None),
        P("row", None, "col"),
        P(ALL, None, None, None),
        P(ALL, None, None),
        P(ALL, None),
        P(ALL, None, None),
    )
    return jax.shard_map(
        local,
        mesh=mesh,
        in_specs=placed,
        out_specs=(P(None, "row", "col"), P(ALL, None, None, None), P(ALL, None, None, None)),
        check_vma=False,
    )
```

time: 876 us -> 290 us (0.33)
  the two profiles are of different devices: /device:TPU:33 before, /device:TPU:1 now
where the time goes in v1:
time: 290 us; the launch traced here: 285 us
  waiting for transfers between devices  186 us (64%)
  starting transfers between devices  37.6 us (13%)
  Pallas kernels  37 us (13%)
  local copies, waits for them, and re-layouts  14.6 us (5%)
  matrix products  6.91 us (2%)
    all_to_all x1, waiting for transfers between devices, local(): lax.all_to_all(outgoing.reshape(PEERS, 64, LANES), ALL, 0, 0, tiled=True)  85.7 us
    ppermute x1, waiting for transfers between devices, padded(): before = lax.ppermute(last, axis, up)  84.3 us
    pallas_call x1, Pallas kernels, local(): pl.pallas_call(grid_kernel, out_shape=jax.ShapeDtypeStruct((TASKS, 1, POI...  14.8 us
    all_to_all x1, starting transfers between devices, local(): lax.all_to_all(potential, 'row', split_axis=1, concat_axis=0, tiled=True)  14.5 us
    pallas_call x1, Pallas kernels, local(): pl.pallas_call(matrix_kernel, out_shape=BLOCKS, grid=(TASKS,), in_specs=[...  12.2 us
    unnamed x13, local copies, waits for them, and re-layouts  11.1 us
    all_to_all x1, waiting for transfers between devices, local(): lax.all_to_all(sent, ALL, 0, 0, tiled=True).reshape(PEERS, LANES)[:, :6]  7.77 us
    all_to_all x1, starting transfers between devices, local(): lax.all_to_all(outgoing.reshape(PEERS, 64, LANES), ALL, 0, 0, tiled=True)  7.54 us
  transfers between devices with their start and end apart: 6, of which 5 were waited for; matrix products, arithmetic and copies ran while one was open for 7% of the time, Pallas kernels for 11%

profile of v1, /device:TPU:1, one launch (start us, length us, event | category | flops | bytes accessed | tf_op | source)
XLA Modules:
  0.0 284.5 jit_solution(11486079462944252017)
XLA Ops:
  0.6 1.4 copy.70
  2.0 14.5 %all-to-all-start.2 = ((f32[1,32,256]{2,0,1:T(1,128)}), f32[1,32,256]{2,0,1:T(1,128)S(1)}, u32[]{:S(2)}, u32[]{:S(2)}) async-start(f32[1,32,256]{2,0,1:T(1,128)} %copy.70), calls=%async_computation.2 | async-start | bytes 65536 | tf_op jit(solution)/shard_map/all_to_all | solution.py:190
  16.5 0.8 fusion.113
  17.3 0.1 copy.64
  17.4 0.1 stack.49
  17.5 0.1 copy.65
  17.6 0.1 stack.50
  17.7 0.8 copy.62
  18.4 0.1 reshape.127
  18.5 0.2 convert_reduce_fusion
  18.7 0.8 copy.63
  19.5 0.1 stack.48
  19.6 0.1 iota_compare_fusion.1
  19.7 0.1 select_reduce_fusion
  19.9 0.3 sub.7
  20.2 0.1 copy.66
  20.4 0.1 copy.87
  20.6 0.8 pad.4.clone
  21.3 6.2 %all-to-all-done.2 = f32[1,32,256]{2,0,1:T(1,128)S(1)} async-done(((f32[1,32,256]{2,0,1:T(1,128)}), f32[1,32,256]{2,0,1:T(1,128)S(1)}, u32[]{:S(2)}, u32[]{:S(2)}) %all-to-all-start.2) | async-done | bytes 32800 | tf_op jit(solution)/shard_map/all_to_all | solution.py:190
  27.6 7.3 %all-to-all-start = ((s32[256,1,128]{2,1,0:T(1,128)}), s32[256,1,128]{2,1,0:T(1,128)S(1)}, u32[]{:S(2)}, u32[]{:S(2)}) async-start(s32[256,1,128]{2,1,0:T(1,128)} %pad.4.clone), calls=%async_computation | async-start | bytes 262144 | tf_op jit(solution)/shard_map/all_to_all | solution.py:175
  34.9 5.0 %pack.1 = bf16[512,32,128]{2,1,0:T(8,128)(2,1)} custom-call(s32[120]{0:T(128)} %copy-done.2, bf16[120,64,64]{2,1,0:T(8,128)(2,1)} %bitcast.102), custom_call_target="tpu_custom_call" | custom-call | bytes 6291456 | tf_op jit(solution)/shard_map/pack/pallas_call | solution.py:179
  39.9 7.8 %all-to-all-done = s32[256,1,128]{2,1,0:T(1,128)S(1)} async-done(((s32[256,1,128]{2,1,0:T(1,128)}), s32[256,1,128]{2,1,0:T(1,128)S(1)}, u32[]{:S(2)}, u32[]{:S(2)}) %all-to-all-start) | async-done | bytes 131104 | tf_op jit(solution)/shard_map/all_to_all | solution.py:175
  47.7 7.5 %all-to-all-start.1 = ((bf16[256,64,128]{2,1,0:T(8,128)(2,1)}), bf16[256,64,128]{2,1,0:T(8,128)(2,1)}, u32[]{:S(2)}, u32[]{:S(2)}) async-start(bf16[256,64,128]{2,1,0:T(8,128)(2,1)} %bitcast.101), calls=%async_computation.1 | async-start | bytes 8388608 | tf_op jit(solution)/shard_map/all_to_all | solution.py:188
  55.3 0.1 copy.68
  55.4 0.1 copy.69
  55.5 0.7 select_n.14.label
  56.2 12.2 %matrices.1 = bf16[512,32,128]{2,1,0:T(8,128)(2,1)} custom-call(s32[512]{0:T(512)} %select_n.14.label, bf16[8,512,1024]{2,1,0:T(8,128)(2,1)} %bitcast.108, f32[8,1,1024]{2,1,0:T(1,128)} %bitcast.107), custom_call_target="tpu_custom_call" | custom-call | flops 4294967296 | bytes 14680064 | tf_op jit(solution)/shard_map/matrices/pallas_call | solution.py:194
  68.5 85.7 %all-to-all-done.1 = bf16[256,64,128]{2,1,0:T(8,128)(2,1)} async-done(((bf16[256,64,128]{2,1,0:T(8,128)(2,1)}), bf16[256,64,128]{2,1,0:T(8,128)(2,1)}, u32[]{:S(2)}, u32[]{:S(2)}) %all-to-all-start.1) | async-done | bytes 4194336 | tf_op jit(solution)/shard_map/all_to_all | solution.py:188
  154.2 6.9 %all-to-all-start.3 = ((bf16[256,64,128]{2,1,0:T(8,128)(2,1)}), bf16[256,64,128]{2,1,0:T(8,128)(2,1)}, u32[]{:S(2)}, u32[]{:S(2)}) async-start(bf16[256,64,128]{2,1,0:T(8,128)(2,1)} %bitcast.103), calls=%async_computation.3 | async-start | bytes 8388608 | tf_op jit(solution)/shard_map/all_to_all | solution.py:212
  161.0 2.8 copy.71
  163.9 0.6 collective-permute-start
  164.5 0.7 collective-permute-start.1
  165.3 84.3 %collective-permute-done = bf16[2,5,64,64]{2,3,1,0:T(8,128)(2,1)S(1)} collective-permute-done((bf16[2,5,64,64]{2,3,1,0:T(8,128)(2,1)S(1)}, bf16[2,5,64,64]{2,3,1,0:T(8,128)(2,1)S(1)}, u32[]{:S(2)}, u32[]{:S(2)}) %collective-permute-start) | collective-permute-done | bytes 81952 | tf_op jit(solution)/shard_map/ppermute | solution.py:31
  249.5 0.1 fusion.103
  249.6 0.5 fusion.97
  250.1 0.1 slice_dynamic-update-slice_fusion
  250.2 1.8 collective-permute-done.1
  251.9 0.4 fusion.88
  252.3 0.4 fusion.111
  252.7 1.1 copy-done
  253.9 1.3 fusion.49
  255.2 1.4 fusion.55
  256.6 1.5 fusion.45
  258.1 1.4 fusion.65
  259.5 1.3 fusion.47
  260.8 4.0 %copy.81 = bf16[24,5,64,64]{3,2,1,0:T(8,128)(2,1)} copy(bf16[24,5,64,64]{2,3,0,1:T(8,128)(2,1)} %fusion.47) | data formatting | bytes 1966080
  264.8 14.8 %collocate.1 = f32[8,1,1024]{2,1,0:T(1,128)} custom-call(s32[512]{0:T(512)} %select_n.14.label, bf16[512,32,128]{2,1,0:T(8,128)(2,1)} %bitcast.4.blocks, bf16[8,512,1024]{2,1,0:T(8,128)(2,1)} %bitcast.109), custom_call_target="tpu_custom_call" | custom-call | flops 4294967296 | bytes 14680064 | tf_op jit(solution)/shard_map/collocate/pallas_call | solution.py:214
  279.6 5.0 %unpack.1 = bf16[120,64,64]{2,1,0:T(8,128)(2,1)} custom-call(s32[120]{0:T(128)} %copy-done.2, bf16[512,32,128]{2,1,0:T(8,128)(2,1)} %bitcast.9.blocks), custom_call_target="tpu_custom_call" | custom-call | bytes 6291456 | tf_op jit(solution)/shard_map/unpack/pallas_call | solution.py:230
  (13 shorter events, 0.1 us)
Async XLA Ops:
  2.0 25.5 %all-to-all-start.2 = ((f32[1,32,256]{2,0,1:T(1,128)}), f32[1,32,256]{2,0,1:T(1,128)S(1)}, u32[]{:S(2)}, u32[]{:S(2)}) async-start(f32[1,32,256]{2,0,1:T(1,128)} %copy.70), calls=%async_computation.2 | async-start | bytes 65536 | tf_op jit(solution)/shard_map/all_to_all | solution.py:190
  18.7 16.2 %copy-start.2 = (s32[120]{0:T(128)}, s32[120]{0:T(128)S(1)}, u32[]{:S(2)}) copy-start(s32[120]{0:T(128)S(1)} %multiply_add_fusion.place) | copy-start | bytes 1444
  27.6 12.4 %copy-start.1 = (f32[1,32,256]{2,0,1:T(1,128)}, f32[1,32,256]{2,0,1:T(1,128)S(1)}, u32[]{:S(2)}) copy-start(f32[1,32,256]{2,0,1:T(1,128)S(1)} %all-to-all-done.2) | copy-start | bytes 98308
  27.6 20.1 %all-to-all-start = ((s32[256,1,128]{2,1,0:T(1,128)}), s32[256,1,128]{2,1,0:T(1,128)S(1)}, u32[]{:S(2)}, u32[]{:S(2)}) async-start(s32[256,1,128]{2,1,0:T(1,128)} %pad.4.clone), calls=%async_computation | async-start | bytes 262144 | tf_op jit(solution)/shard_map/all_to_all | solution.py:175
  47.7 106.4 %all-to-all-start.1 = ((bf16[256,64,128]{2,1,0:T(8,128)(2,1)}), bf16[256,64,128]{2,1,0:T(8,128)(2,1)}, u32[]{:S(2)}, u32[]{:S(2)}) async-start(bf16[256,64,128]{2,1,0:T(8,128)(2,1)} %bitcast.101), calls=%async_computation.1 | async-start | bytes 8388608 | tf_op jit(solution)/shard_map/all_to_all | solution.py:188
  154.2 125.4 %all-to-all-start.3 = ((bf16[256,64,128]{2,1,0:T(8,128)(2,1)}), bf16[256,64,128]{2,1,0:T(8,128)(2,1)}, u32[]{:S(2)}, u32[]{:S(2)}) async-start(bf16[256,64,128]{2,1,0:T(8,128)(2,1)} %bitcast.103), calls=%async_computation.3 | async-start | bytes 8388608 | tf_op jit(solution)/shard_map/all_to_all | solution.py:212
  163.9 85.6 %collective-permute-start = (bf16[2,5,64,64]{2,3,1,0:T(8,128)(2,1)S(1)}, bf16[2,5,64,64]{2,3,1,0:T(8,128)(2,1)S(1)}, u32[]{:S(2)}, u32[]{:S(2)}) collective-permute-start(bf16[2,5,64,64]{2,3,1,0:T(8,128)(2,1)S(1)} %get-tuple-element.31), channel_id=1, source_target_pairs={{0,1},{1,2},{2,3},{3,4},{4,5},{5,6},{6,7},{7,8},{8,9},{9,10},{10,1... | collective-permute-start | bytes 245768 | tf_op jit(solution)/shard_map/ppermute | solution.py:31
  164.5 87.4 %collective-permute-start.1 = (bf16[2,5,64,64]{2,3,1,0:T(8,128)(2,1)S(1)}, bf16[2,5,64,64]{2,3,1,0:T(8,128)(2,1)S(1)}, u32[]{:S(2)}, u32[]{:S(2)}) collective-permute-start(bf16[2,5,64,64]{2,3,1,0:T(8,128)(2,1)S(1)} %get-tuple-element.30), channel_id=1, source_target_pairs={{1,0},{2,1},{3,2},{4,3},{5,4},{6,5},{7,6},{8,7},{9,8},{10,9},{11,1... | collective-permute-start | bytes 245768 | tf_op jit(solution)/shard_map/ppermute | solution.py:32
  252.3 1.5 copy-start

commit v2 on v1

--- a/solution.py
+++ b/solution.py
@@ -18,6 +18,11 @@
 BASIS = 512
 POINTS = 1024
 ALL = ("row", "col")
+ZS = 8
+PLANE = 32
+CAP = 32
+HELD = ZS * CAP
+MESH = pl.DeviceIdType.MESH
 VMEM_LIMIT = 56 * 1024 * 1024
 
 
@@ -74,6 +79,99 @@
         return carry
 
     lax.fori_loop(0, PAIRS // 8, body, 0)
+
+
+def exchange_kernel(zsend, psend, zrecv, precv, zs, zr, ps, pr, own):
+    row, col = lax.axis_index("row"), lax.axis_index("col")
+    y, x, high = row // 8, lax.rem(row // 2, 4), lax.rem(row, 2)
+    low, core = col // 2, lax.rem(col, 2)
+    z = high * 4 + low
+    here = (y * 4 + x) * 2 + core
+
+    def along(step):
+        to = lax.rem(z + step, ZS)
+        return to, (y * 8 + x * 2 + to // 4, lax.rem(to, 4) * 2 + core)
+
+    def across(dy, dx, dc):
+        to_y, to_x, to_c = lax.rem(y + dy, 4), lax.rem(x + dx, 4), lax.rem(core + dc, 2)
+        return (to_y * 4 + to_x) * 2 + to_c, (to_y * 8 + to_x * 2 + high, low * 2 + to_c)
+
+    zsteps = (4, 3, 5, 2, 6, 1, 7)
+    psteps = [
+        (dy, dx, dc)
+        for dy, dx in (
+            (2, 2), (1, 3), (3, 1), (1, 1), (3, 3), (2, 1), (2, 3), (1, 2), (3, 2), (0, 2), (2, 0), (0, 1), (0, 3), (1, 0), (3, 0), (0, 0),
+        )
+        for dc in (0, 1)
+        if (dy, dx, dc) != (0, 0, 0)
+    ]
+    barrier = pltpu.get_barrier_semaphore()
+    for step in zsteps:
+        pl.semaphore_signal(barrier, inc=1, device_id=along(step)[1], device_id_type=MESH)
+    for steps in psteps:
+        pl.semaphore_signal(barrier, inc=1, device_id=across(*steps)[1], device_id_type=MESH)
+    pl.semaphore_wait(barrier, len(zsteps) + len(psteps))
+    copies = []
+    for number in range(len(psteps)):
+        if number < len(zsteps):
+            to, where = along(zsteps[number])
+            copies.append(
+                pltpu.make_async_remote_copy(
+                    src_ref=zsend.at[to], dst_ref=zrecv.at[z], send_sem=zs.at[number], recv_sem=zr.at[number],
+                    device_id=where, device_id_type=MESH,
+                )
+            )
+            copies[-1].start()
+        to, where = across(*psteps[number])
+        copies.append(
+            pltpu.make_async_remote_copy(
+                src_ref=psend.at[to], dst_ref=precv.at[here], send_sem=ps.at[number], recv_sem=pr.at[number],
+                device_id=where, device_id_type=MESH,
+            )
+        )
+        copies[-1].start()
+    mine = [
+        pltpu.make_async_copy(zsend.at[z], zrecv.at[z], own.at[0]),
+        pltpu.make_async_copy(psend.at[here], precv.at[here], own.at[1]),
+    ]
+    for copy in mine:
+        copy.start()
+    for copy in mine + copies:
+        copy.wait()
+
+
+def exchange(zsend, psend, number):
+    hbm = pl.BlockSpec(memory_space=pl.ANY)
+    return pl.pallas_call(
+        exchange_kernel,
+        out_shape=(
+            jax.ShapeDtypeStruct((ZS, CAP * ROWS, LANES), jnp.bfloat16),
+            jax.ShapeDtypeStruct((PLANE, 16 * ROWS, LANES), jnp.bfloat16),
+        ),
+        in_specs=[hbm, hbm],
+        out_specs=(hbm, hbm),
+        scratch_shapes=[
+            pltpu.SemaphoreType.DMA((7,)),
+            pltpu.SemaphoreType.DMA((7,)),
+            pltpu.SemaphoreType.DMA((31,)),
+            pltpu.SemaphoreType.DMA((31,)),
+            pltpu.SemaphoreType.DMA((2,)),
+        ],
+        compiler_params=params(collective_id=number, has_side_effects=True),
+        name="exchange",
+    )(zsend, psend)
+
+
+def swap_kernel(spot, held, results, out, back):
+    def body(step, carry):
+        for inner in range(8):
+            item = step * 8 + inner
+            where = spot[item]
+            out[where] = held[item]
+            back[item] = results[jnp.minimum(where, SLOTS_ALL - 1)]
+        return carry
+
+    lax.fori_loop(0, HELD // 8, body, 0)
 
 
 def matrix_kernel(label, basis, potential, out, scaled, table):
@@ -151,6 +249,7 @@
 
 
 SMEM = pl.BlockSpec(memory_space=pltpu.SMEM)
+VM = pl.BlockSpec(memory_space=pltpu.VMEM)
 BLOCKS = jax.ShapeDtypeStruct((SLOTS_ALL, ROWS, LANES), jnp.bfloat16)
 
 
@@ -158,39 +257,97 @@
     return pl.BlockSpec(shape, lambda *_: (0,) * len(shape))
 
 
+def packed(places, flat, blocks):
+    return pl.pallas_call(
+        pack_kernel,
+        out_shape=jax.ShapeDtypeStruct((blocks, ROWS, LANES), jnp.bfloat16),
+        in_specs=[SMEM, VM],
+        out_specs=VM,
+        compiler_params=params(),
+        cost_estimate=pl.CostEstimate(flops=0, bytes_accessed=6 << 20, transcendentals=0),
+        name="pack",
+    )(places, flat)
+
+
+def unpacked(places, blocks):
+    return pl.pallas_call(
+        unpack_kernel,
+        out_shape=jax.ShapeDtypeStruct((PAIRS, BF, BF), jnp.bfloat16),
+        in_specs=[SMEM, VM],
+        out_specs=VM,
+        compiler_params=params(),
+        cost_estimate=pl.CostEstimate(flops=0, bytes_accessed=6 << 20, transcendentals=0),
+        name="unpack",
+    )(places, blocks)
+
+
+def swapped(spot, held, results):
+    return pl.pallas_call(
+        swap_kernel,
+        out_shape=(
+            jax.ShapeDtypeStruct((SLOTS_ALL + 16, ROWS, LANES), jnp.bfloat16),
+            jax.ShapeDtypeStruct((HELD, ROWS, LANES), jnp.bfloat16),
+        ),
+        in_specs=[SMEM, VM, VM],
+        out_specs=(VM, VM),
+        compiler_params=params(),
+        name="swap",
+    )(spot, held, results)
+
+
+def by_plane(values):
+    rest = values.shape[1:]
+    return values.reshape((16, 8, 2) + rest).swapaxes(1, 2).reshape((PEERS,) + rest)
+
+
+def by_mesh(values):
+    rest = values.shape[1:]
+    return values.reshape((16, 2, 8) + rest).swapaxes(1, 2).reshape((PEERS,) + rest)
+
+
 def local(density, margin, potential, basis_values, pair_owner, pair_box, pair_slots):
     atoms_here, offsets = density.shape[:2]
+    row, col = lax.axis_index("row"), lax.axis_index("col")
     owners = pair_owner.reshape(PAIRS)
-    same = owners[:, None] == owners[None, :]
+    planes = (owners // 8) % 2 * 4 + owners % 8 // 2
+    inside = owners // 16 * 2 + owners % 2
     before = jnp.arange(PAIRS)[:, None] > jnp.arange(PAIRS)[None, :]
-    ranks = jnp.sum((same & before).astype(jnp.int32), axis=1)
+    ranks = jnp.sum(((owners[:, None] == owners[None, :]) & before).astype(jnp.int32), axis=1)
+    turns = jnp.sum(((planes[:, None] == planes[None, :]) & before).astype(jnp.int32), axis=1)
     places = owners * 2 + ranks
+    spots = jnp.where(turns < CAP, planes * CAP + turns, HELD)
+    flat = density.reshape(PAIRS, BF, BF)
+    held = packed(spots, flat, HELD + CAP)
+
     fields = jnp.stack(
         [pair_box.reshape(PAIRS), pair_slots[..., 0].reshape(PAIRS), pair_slots[..., 1].reshape(PAIRS)], axis=0
     )
     chosen = jnp.arange(SLOTS_ALL, dtype=jnp.int32)[None, :, None] == places[None, None, :]
-    sent = jnp.sum(jnp.where(chosen, fields[:, None, :] + 1, 0), axis=2) - 1
-    sent = sent.reshape(3, PEERS, 2).transpose(1, 0, 2).reshape(PEERS, 1, 6)
-    sent = jnp.pad(sent, ((0, 0), (0, 0), (0, LANES - 6)))
-    tags = lax.all_to_all(sent, ALL, 0, 0, tiled=True).reshape(PEERS, LANES)[:, :6].reshape(PEERS, 3, 2)
+    tags = jnp.sum(jnp.where(chosen, fields[:, None, :] + 1, 0), axis=2) - 1
+    tags = tags.reshape(3, PEERS, 2).transpose(1, 0, 2).reshape(PEERS, 6)
+    listed = jnp.arange(HELD, dtype=jnp.int32)[:, None] == spots[None, :]
+    targets = jnp.sum(jnp.where(listed, (inside * 2 + ranks)[None, :] + 1, 0), axis=1) - 1
+    targets = jnp.broadcast_to(targets.reshape(1, ZS, 1, CAP), (16, ZS, 2, CAP)).reshape(PEERS, CAP)
+    over = jnp.max(turns) >= CAP
+    rows = jnp.broadcast_to(potential[0][:, None, :], (32, 8, 256)).reshape(PEERS, 256)
+    notes = jnp.concatenate(
+        [tags, jnp.broadcast_to(over.astype(jnp.int32), (PEERS, 2)), targets, jnp.zeros((PEERS, LANES - 8 - CAP), jnp.int32)],
+        axis=1,
+    ).astype(jnp.float32)
+    sent = jnp.concatenate([notes, rows], axis=1).reshape(PEERS, 1, LANES + 256)
+    got = lax.all_to_all(sent, ALL, 0, 0, tiled=True).reshape(PEERS, LANES + 256)
+    notes = got[:, :LANES].astype(jnp.int32)
+    pencil = lax.dynamic_index_in_dim(got[:, LANES:].reshape(32, 8, 256), col, 1, keepdims=False)
+    box_potential = pencil.reshape(TASKS, 1, POINTS)
+    over = jnp.max(notes[:, 6]) > 0
+    tags = by_plane(notes[:, :6]).reshape(PEERS, 3, 2)
     labels = jnp.where(tags[:, 0] < 0, -1, tags[:, 0] * 64 + tags[:, 1] * 8 + tags[:, 2]).reshape(SLOTS_ALL)
-
-    flat = density.reshape(PAIRS, BF, BF)
-    outgoing = pl.pallas_call(
-        pack_kernel,
-        out_shape=BLOCKS,
-        in_specs=[SMEM, pl.BlockSpec(memory_space=pltpu.VMEM)],
-        out_specs=pl.BlockSpec(memory_space=pltpu.VMEM),
-        compiler_params=params(),
-        cost_estimate=pl.CostEstimate(flops=0, bytes_accessed=6 << 20, transcendentals=0),
-        name="pack",
-    )(places, flat)
-    arrived = lax.all_to_all(outgoing.reshape(PEERS, 64, LANES), ALL, 0, 0, tiled=True).reshape(BLOCKS.shape)
-
-    pencil = lax.all_to_all(potential, "row", split_axis=1, concat_axis=0, tiled=True)
-    box_potential = pencil.reshape(TASKS, 1, POINTS)
+    here = row // 2 * 2 + col % 2
+    targets = lax.dynamic_index_in_dim(by_plane(notes[:, 8 : 8 + CAP]).reshape(PLANE, ZS, CAP), here, 0, keepdims=False)
+    number = jnp.arange(HELD, dtype=jnp.int32).reshape(ZS, CAP)
+    routes = jnp.where(targets < 0, SLOTS_ALL + number % 16, targets // 2 * 16 + number // CAP * 2 + targets % 2).reshape(HELD)
+
     phi = basis_values.reshape(TASKS, BASIS, POINTS)
-
     results = pl.pallas_call(
         matrix_kernel,
         out_shape=BLOCKS,
@@ -209,7 +366,23 @@
         cost_estimate=pl.CostEstimate(flops=2 * TASKS * BASIS * BASIS * POINTS, bytes_accessed=14 << 20, transcendentals=0),
         name="matrices",
     )(labels, phi, box_potential)
-    returned = lax.all_to_all(results.reshape(PEERS, 64, LANES), ALL, 0, 0, tiled=True).reshape(BLOCKS.shape)
+
+    margin_product = margin_of(density, margin)
+    results, margin_product = lax.optimization_barrier((results, margin_product))
+
+    def fast(results, held, flat, places, spots, routes):
+        got_z, got_p = exchange(held.reshape(ZS + 1, CAP * ROWS, LANES), results.reshape(PLANE, 16 * ROWS, LANES), 0)
+        out, back = swapped(routes, got_z.reshape(HELD, ROWS, LANES), got_p.reshape(BLOCKS.shape))
+        back, arrived = exchange(back.reshape(ZS, CAP * ROWS, LANES), out.reshape(PLANE + 1, 16 * ROWS, LANES), 1)
+        return arrived.reshape(BLOCKS.shape), unpacked(spots, back.reshape(HELD, ROWS, LANES))
+
+    def dense(results, held, flat, places, spots, routes):
+        outgoing = packed(places, flat, SLOTS_ALL)
+        arrived = by_plane(lax.all_to_all(outgoing.reshape(PEERS, 64, LANES), ALL, 0, 0, tiled=True))
+        returned = lax.all_to_all(by_mesh(results.reshape(PEERS, 64, LANES)), ALL, 0, 0, tiled=True)
+        return arrived.reshape(BLOCKS.shape), unpacked(places, returned.reshape(BLOCKS.shape))
+
+    arrived, ks_blocks = lax.cond(over, dense, fast, results, held, flat, places, spots, routes)
 
     grid_rows = pl.pallas_call(
         grid_kernel,
@@ -225,18 +398,8 @@
         cost_estimate=pl.CostEstimate(flops=2 * TASKS * BASIS * BASIS * POINTS, bytes_accessed=14 << 20, transcendentals=0),
         name="collocate",
     )(labels, arrived, phi)
-    density_grid = grid_rows.reshape(pencil.shape)
-
-    ks_blocks = pl.pallas_call(
-        unpack_kernel,
-        out_shape=jax.ShapeDtypeStruct((PAIRS, BF, BF), jnp.bfloat16),
-        in_specs=[SMEM, pl.BlockSpec(memory_space=pltpu.VMEM)],
-        out_specs=pl.BlockSpec(memory_space=pltpu.VMEM),
-        compiler_params=params(),
-        cost_estimate=pl.CostEstimate(flops=0, bytes_accessed=6 << 20, transcendentals=0),
-        name="unpack",
-    )(places, returned).reshape(atoms_here, offsets, BF, BF)
-    return density_grid, ks_blocks, margin_of(density, margin)
+    density_grid = grid_rows.reshape(32, 1, 256)
+    return density_grid, ks_blocks.reshape(atoms_here, offsets, BF, BF), margin_product
 
 
 def solution(mesh):

time: 290 us -> 210 us (0.72); the launches traced: 285 us -> 208 us
  waiting for transfers between devices: 186 us -> 3.9 us
  Pallas kernels: 37 us -> 159 us
  starting transfers between devices: 37.6 us -> 18.7 us
    pallas_call x2 -> x5, Pallas kernels: 10 us -> 134 us  [the longest x2 120 us: exchange(): pl.pallas_call(exchange_kernel, out_shape=(jax.ShapeDtypeStruct((ZS, CAP...]
    all_to_all x4 -> x1, waiting for transfers between devices: 99.7 us -> 0.01 us  [local(): lax.all_to_all(sent, ALL, 0, 0, tiled=True).reshape(PEERS, LANES + 256)]
    ppermute x1, waiting for transfers between devices: 84.3 us -> 0.01 us  [padded(): before = lax.ppermute(last, axis, up)]
    all_to_all x4 -> x1, starting transfers between devices: 36.2 us -> 13.4 us  [local(): lax.all_to_all(sent, ALL, 0, 0, tiled=True).reshape(PEERS, LANES + 256)]
    unnamed x13 -> x22, local copies, waits for them, and re-layouts: 11.1 us -> 8.39 us
  transfers between devices with their start and end apart: 6 -> 3, of which waited for: 5 -> 1; matrix products, arithmetic and copies ran while one was open for 7% -> 6% of each run, Pallas kernels for 11% -> 2%
where the time goes in v2:
time: 210 us; the launch traced here: 208 us
  Pallas kernels  159 us (76%)
  starting transfers between devices  18.7 us (9%)
  local copies, waits for them, and re-layouts  13.2 us (6%)
  matrix products  6.91 us (3%)
  other arithmetic  4.21 us (2%)
  waiting for transfers between devices  3.9 us (2%)
  between operations  2.26 us (1%)
    pallas_call x2, Pallas kernels, exchange(): pl.pallas_call(exchange_kernel, out_shape=(jax.ShapeDtypeStruct((ZS, CAP...  120 us
    all_to_all x1, starting transfers between devices, local(): lax.all_to_all(sent, ALL, 0, 0, tiled=True).reshape(PEERS, LANES + 256)  13.4 us
    pallas_call x1, Pallas kernels, local(): pl.pallas_call(grid_kernel, out_shape=jax.ShapeDtypeStruct((TASKS, 1, POI...  13.2 us
    pallas_call x1, Pallas kernels, local(): pl.pallas_call(matrix_kernel, out_shape=BLOCKS, grid=(TASKS,), in_specs=[...  12.3 us
    unnamed x22, local copies, waits for them, and re-layouts  8.39 us
    dot_general x5, matrix products, margin_of(): jnp.einsum('amik,amkj->aij', left_blocks, right_blocks, preferred_element...  6.91 us
    pallas_call x1, Pallas kernels, swapped(): pl.pallas_call(swap_kernel, out_shape=(jax.ShapeDtypeStruct((SLOTS_ALL +...  6.25 us
    pallas_call x1, Pallas kernels, packed(): pl.pallas_call(pack_kernel, out_shape=jax.ShapeDtypeStruct((blocks, ROWS,...  4.48 us
  transfers between devices with their start and end apart: 3, of which 1 were waited for; matrix products, arithmetic and copies ran while one was open for 6% of the time, Pallas kernels for 2%

profile of v2, /device:TPU:1, one launch (start us, length us, event | category | flops | bytes accessed | tf_op | source)
XLA Modules:
  0.0 208.5 jit_solution(559070744944335239)
XLA Ops:
  0.7 2.8 %copy.103 = bf16[24,5,64,64]{2,3,1,0:T(8,128)(2,1)S(1)} copy(bf16[24,5,64,64]{3,2,1,0:T(8,128)(2,1)} %param.10) | data formatting | bytes 1966080 | tf_op args[1]
  3.6 3.1 %collective-permute-start = (bf16[2,5,64,64]{2,3,1,0:T(8,128)(2,1)S(1)}, bf16[2,5,64,64]{2,3,1,0:T(8,128)(2,1)S(1)}, u32[]{:S(2)}, u32[]{:S(2)}) collective-permute-start(bf16[2,5,64,64]{2,3,1,0:T(8,128)(2,1)S(1)} %get-tuple-element.221), channel_id=1, source_target_pairs={{0,1},{1,2},{2,3},{3,4},{4,5},{5,6},{6,7},{7,8},{8,9},{9,10},{10,1... | collective-permute-start | bytes 245768 | tf_op jit(solution)/shard_map/ppermute | solution.py:36
  6.7 0.1 copy.96
  6.8 0.1 stack.49
  7.0 0.1 stack.50
  7.2 0.1 reshape.424
  7.3 0.2 convert_reduce_fusion.1
  7.5 0.2 convert_reduce_fusion
  7.7 0.6 fusion.121
  9.1 0.1 select_reduce_fusion.1
  9.4 0.1 stack.48
  9.5 0.1 iota_compare_fusion.1
  9.6 0.1 select_reduce_fusion
  9.8 0.3 sub.41
  10.1 0.1 copy.98
  10.3 0.1 copy.99
  10.5 0.1 add_convert_fusion
  10.7 1.0 reshape.428
  11.7 13.4 %all-to-all-start.2 = ((f32[256,1,384]{2,1,0:T(1,128)}), f32[256,1,384]{2,1,0:T(1,128)S(1)}, u32[]{:S(2)}, u32[]{:S(2)}) async-start(f32[256,1,384]{2,1,0:T(1,128)} %reshape.428), calls=%async_computation.2 | async-start | bytes 786432 | tf_op jit(solution)/shard_map/all_to_all | solution.py:338
  25.0 2.2 %collective-permute-start.1 = (bf16[2,5,64,64]{2,3,1,0:T(8,128)(2,1)S(1)}, bf16[2,5,64,64]{2,3,1,0:T(8,128)(2,1)S(1)}, u32[]{:S(2)}, u32[]{:S(2)}) collective-permute-start(bf16[2,5,64,64]{2,3,1,0:T(8,128)(2,1)S(1)} %get-tuple-element.220), channel_id=1, source_target_pairs={{1,0},{2,1},{3,2},{4,3},{5,4},{6,5},{7,6},{8,7},{9,8},{10,9},{11,1... | collective-permute-start | bytes 245768 | tf_op jit(solution)/shard_map/ppermute | solution.py:37
  27.3 4.5 %pack.3 = bf16[288,32,128]{2,1,0:T(8,128)(2,1)} custom-call(s32[120]{0:T(128)S(1)} %get-tuple-element.227.place, bf16[120,64,64]{2,1,0:T(8,128)(2,1)} %bitcast.131), custom_call_target="tpu_custom_call" | custom-call | bytes 6291456 | tf_op jit(solution)/shard_map/pack/pallas_call | solution.py:261
  31.8 0.1 fusion.105
  31.9 0.5 fusion.99
  32.4 3.9 %collective-permute-done.1 = bf16[2,5,64,64]{2,3,1,0:T(8,128)(2,1)S(1)} collective-permute-done((bf16[2,5,64,64]{2,3,1,0:T(8,128)(2,1)S(1)}, bf16[2,5,64,64]{2,3,1,0:T(8,128)(2,1)S(1)}, u32[]{:S(2)}, u32[]{:S(2)}) %collective-permute-start.1) | collective-permute-done | bytes 81952 | tf_op jit(solution)/shard_map/ppermute | solution.py:37
  36.3 0.4 fusion.90
  36.7 0.4 fusion.118
  37.1 1.1 copy-done.2
  38.2 1.3 fusion.51
  39.5 1.4 fusion.57
  40.9 1.5 fusion.47
  42.4 1.4 fusion.67
  43.8 1.3 fusion.49
  45.2 0.7 slice_reduce_fusion
  46.0 0.1 slice.161
  46.7 0.3 copy.100
  47.1 0.2 reshape_reshape.6
  47.2 0.1 copy.101
  47.4 0.7 select_n.157.label
  48.1 0.6 constant_dynamic-slice_fusion.1
  48.8 12.3 %matrices.1 = bf16[512,32,128]{2,1,0:T(8,128)(2,1)} custom-call(s32[512]{0:T(512)} %select_n.157.label, bf16[8,512,1024]{2,1,0:T(8,128)(2,1)} %bitcast.154, f32[8,1,1024]{2,1,0:T(1,128)} %bitcast.153), custom_call_target="tpu_custom_call" | custom-call | flops 4294967296 | bytes 14680064 | tf_op jit(solution)/shard_map/matrices/pallas_call | solution.py:351
  61.1 4.1 %copy.113 = bf16[24,5,64,64]{3,2,1,0:T(8,128)(2,1)} copy(bf16[24,5,64,64]{2,3,0,1:T(8,128)(2,1)} %fusion.49) | data formatting | bytes 1966080
  65.2 130.0 %conditional.1 = (bf16[512,32,128]{2,1,0:T(8,128)(2,1)S(1)}, bf16[24,5,64,64]{3,2,1,0:T(8,128)(2,1)S(1)}) conditional(s32[]{:T(128)} %convert_element_type.24, (s32[8,32]{1,0:T(8,128)S(1)}, (), (), s32[]{:T(128)}, s32[32,8,32]{2,1,0:T(8,128)S(1)}, /*index=5*/(), (), bf16[288,32,128]{2,1,0:T(8,128)(2,1)}, bf16[512,32,128]{2,1,0:T(8,128)(2,1)}, ...), branch_computations={%region_6.7_spmd, %region_7.8_spmd} | conditional | flops 13059 | bytes 71304720 | solution.py:385
  65.6 0.6 fusion.1.spot
  66.2 60.9 %exchange.2 = (bf16[8,1024,128]{2,1,0:T(8,128)(2,1)}, bf16[32,512,128]{2,1,0:T(8,128)(2,1)}) custom-call(bf16[9,1024,128]{2,1,0:T(8,128)(2,1)} %bitcast.137, bf16[32,512,128]{2,1,0:T(8,128)(2,1)} %bitcast.133), custom_call_target="tpu_custom_call" | custom-call | tf_op jit(solution)/shard_map/cond/branch_0_fun/exchange/pallas_call | solution.py:145
  127.0 6.2 %swap.1 = (bf16[528,32,128]{2,1,0:T(8,128)(2,1)}, bf16[256,32,128]{2,1,0:T(8,128)(2,1)}) custom-call(s32[256]{0:T(256)} %fusion.1.spot, bf16[256,32,128]{2,1,0:T(8,128)(2,1)} %bitcast.141, bf16[512,32,128]{2,1,0:T(8,128)(2,1)} %bitcast.139), custom_call_target="tpu_custom_call" | custom-call | tf_op jit(solution)/shard_map/cond/branch_0_fun/swap/pallas_call | solution.py:285
  133.3 58.8 %exchange.3 = (bf16[8,1024,128]{2,1,0:T(8,128)(2,1)}, bf16[32,512,128]{2,1,0:T(8,128)(2,1)S(1)}) custom-call(bf16[8,1024,128]{2,1,0:T(8,128)(2,1)} %bitcast.140, bf16[33,512,128]{2,1,0:T(8,128)(2,1)} %bitcast.138), custom_call_target="tpu_custom_call" | custom-call | tf_op jit(solution)/shard_map/cond/branch_0_fun/exchange/pallas_call | solution.py:145
  192.1 3.1 %unpack.2 = bf16[120,64,64]{2,1,0:T(8,128)(2,1)S(1)} custom-call(s32[120]{0:T(128)S(1)} %get-tuple-element.151.place, bf16[256,32,128]{2,1,0:T(8,128)(2,1)} %bitcast.142), custom_call_target="tpu_custom_call" | custom-call | bytes 6291456 | tf_op jit(solution)/shard_map/cond/branch_0_fun/unpack/pallas_call | solution.py:273
  195.2 13.2 %collocate.1 = f32[8,1,1024]{2,1,0:T(1,128)} custom-call(s32[512]{0:T(512)} %select_n.157.label, bf16[512,32,128]{2,1,0:T(8,128)(2,1)S(1)} %get-tuple-element.165.blocks, bf16[8,512,1024]{2,1,0:T(8,128)(2,1)} %bitcast.155), custom_call_target="tpu_custom_call" | custom-call | flops 4294967296 | bytes 14680064 | tf_op jit(solution)/shard_map/collocate/pallas_call | solution.py:387
  (47 shorter events, 1.0 us)
Async XLA Ops:
  0.6 9.1 %copy-start = (f32[1,32,256]{2,1,0:T(8,128)S(1)}, f32[1,32,256]{2,1,0:T(8,128)}, u32[]{:S(2)}) copy-start(f32[1,32,256]{2,1,0:T(8,128)} %param.11) | copy-start | bytes 98308
  0.6 6.1 %copy-start.5 = (s32[24,5,2]{0,2,1:T(2,128)S(1)}, s32[24,5,2]{0,2,1:T(2,128)}, u32[]{:S(2)}) copy-start(s32[24,5,2]{0,2,1:T(2,128)} %param.15) | copy-start | bytes 2884
  0.7 6.5 %copy-start.7 = (s32[24,5,1]{0,2,1:T(1,128)S(1)}, s32[24,5,1]{0,2,1:T(1,128)}, u32[]{:S(2)}) copy-start(s32[24,5,1]{0,2,1:T(1,128)} %param.13) | copy-start | bytes 1444
  0.7 8.6 %copy-start.6 = (s32[24,5]{0,1:T(8,128)S(1)}, s32[24,5]{0,1:T(8,128)}, u32[]{:S(2)}) copy-start(s32[24,5]{0,1:T(8,128)} %param.14) | copy-start | bytes 1444
  3.6 28.2 %collective-permute-start = (bf16[2,5,64,64]{2,3,1,0:T(8,128)(2,1)S(1)}, bf16[2,5,64,64]{2,3,1,0:T(8,128)(2,1)S(1)}, u32[]{:S(2)}, u32[]{:S(2)}) collective-permute-start(bf16[2,5,64,64]{2,3,1,0:T(8,128)(2,1)S(1)} %get-tuple-element.221), channel_id=1, source_target_pairs={{0,1},{1,2},{2,3},{3,4},{4,5},{5,6},{6,7},{7,8},{8,9},{9,10},{10,1... | collective-permute-start | bytes 245768 | tf_op jit(solution)/shard_map/ppermute | solution.py:36
  11.7 33.5 %all-to-all-start.2 = ((f32[256,1,384]{2,1,0:T(1,128)}), f32[256,1,384]{2,1,0:T(1,128)S(1)}, u32[]{:S(2)}, u32[]{:S(2)}) async-start(f32[256,1,384]{2,1,0:T(1,128)} %reshape.428), calls=%async_computation.2 | async-start | bytes 786432 | tf_op jit(solution)/shard_map/all_to_all | solution.py:338
  25.0 11.2 %collective-permute-start.1 = (bf16[2,5,64,64]{2,3,1,0:T(8,128)(2,1)S(1)}, bf16[2,5,64,64]{2,3,1,0:T(8,128)(2,1)S(1)}, u32[]{:S(2)}, u32[]{:S(2)}) collective-permute-start(bf16[2,5,64,64]{2,3,1,0:T(8,128)(2,1)S(1)} %get-tuple-element.220), channel_id=1, source_target_pairs={{1,0},{2,1},{3,2},{4,3},{5,4},{6,5},{7,6},{8,7},{9,8},{10,9},{11,1... | collective-permute-start | bytes 245768 | tf_op jit(solution)/shard_map/ppermute | solution.py:37
  36.7 1.5 copy-start.2
  61.1 4.1 %copy-start.3 = (bf16[24,5,64,64]{3,2,1,0:T(8,128)(2,1)S(1)}, bf16[24,5,64,64]{3,2,1,0:T(8,128)(2,1)}, u32[]{:S(2)}) copy-start(bf16[24,5,64,64]{3,2,1,0:T(8,128)(2,1)} %param.9) | copy-start | bytes 2949124
  195.2 13.3 %copy-start.4 = (bf16[24,5,64,64]{3,2,1,0:T(8,128)(2,1)}, bf16[24,5,64,64]{3,2,1,0:T(8,128)(2,1)S(1)}, u32[]{:S(2)}) copy-start(bf16[24,5,64,64]{3,2,1,0:T(8,128)(2,1)S(1)} %get-tuple-element.186) | copy-start | bytes 2949124
  195.2 13.3 %copy-start.1 = (f32[1,32,256]{2,1,0:T(8,128)S(1)}, f32[1,32,256]{2,1,0:T(8,128)}, u32[]{:S(2)}) copy-start(f32[1,32,256]{2,1,0:T(8,128)} %param.11) | copy-start | bytes 98308

commit v3 on v2

--- a/solution.py
+++ b/solution.py
@@ -69,109 +69,192 @@
     lax.fori_loop(0, PAIRS // 8, body, 0)
 
 
-def unpack_kernel(place, blocks, out):
-    def body(step, carry):
-        for inner in range(8):
-            pair = step * 8 + inner
-            block = blocks[place[pair]]
-            out[pair, 0:ROWS] = block[:, 0:BF]
-            out[pair, ROWS:BF] = block[:, BF:LANES]
-        return carry
-
-    lax.fori_loop(0, PAIRS // 8, body, 0)
-
-
-def exchange_kernel(zsend, psend, zrecv, precv, zs, zr, ps, pr, own):
+PSTEPS = [
+    (dy, dx, dc)
+    for dy, dx in (
+        (2, 2), (1, 3), (3, 1), (1, 1), (3, 3), (2, 1), (2, 3), (1, 2), (3, 2), (0, 2), (2, 0), (0, 1), (0, 3), (1, 0), (3, 0), (0, 0),
+    )
+    for dc in (0, 1)
+    if (dy, dx, dc) != (0, 0, 0)
+]
+ZSTEPS = (4, 3, 5, 2, 6, 1, 7)
+WIDE = 640
+
+
+def exchange_kernel(
+    inverse, routes, held, results, density, margin, arrived, back, product,
+    zgot, pgot, zput, pput, dens, marg, even, odd, zs, zr, ps, pr, zs2, zr2, ps2, pr2, hs, hr, own,
+):
     row, col = lax.axis_index("row"), lax.axis_index("col")
     y, x, high = row // 8, lax.rem(row // 2, 4), lax.rem(row, 2)
     low, core = col // 2, lax.rem(col, 2)
     z = high * 4 + low
     here = (y * 4 + x) * 2 + core
+    flat = row * 8 + col
+    after, before = lax.rem(flat + 1, PEERS), lax.rem(flat + PEERS - 1, PEERS)
+    after, before = (after // 8, lax.rem(after, 8)), (before // 8, lax.rem(before, 8))
 
     def along(step):
         to = lax.rem(z + step, ZS)
         return to, (y * 8 + x * 2 + to // 4, lax.rem(to, 4) * 2 + core)
 
-    def across(dy, dx, dc):
+    def across(steps):
+        dy, dx, dc = steps
         to_y, to_x, to_c = lax.rem(y + dy, 4), lax.rem(x + dx, 4), lax.rem(core + dc, 2)
         return (to_y * 4 + to_x) * 2 + to_c, (to_y * 8 + to_x * 2 + high, low * 2 + to_c)
 
-    zsteps = (4, 3, 5, 2, 6, 1, 7)
-    psteps = [
-        (dy, dx, dc)
-        for dy, dx in (
-            (2, 2), (1, 3), (3, 1), (1, 1), (3, 3), (2, 1), (2, 3), (1, 2), (3, 2), (0, 2), (2, 0), (0, 1), (0, 3), (1, 0), (3, 0), (0, 0),
+    def send(source, target, sent, received, where):
+        copy = pltpu.make_async_remote_copy(
+            src_ref=source, dst_ref=target, send_sem=sent, recv_sem=received, device_id=where, device_id_type=MESH
         )
-        for dc in (0, 1)
-        if (dy, dx, dc) != (0, 0, 0)
+        copy.start()
+        return copy
+
+    def keep(source, target, semaphore):
+        copy = pltpu.make_async_copy(source, target, semaphore)
+        copy.start()
+        return copy
+
+    def rows(ref, start, count):
+        return ref.at[pl.ds(start * count, count)]
+
+    barrier = pltpu.get_barrier_semaphore()
+    for step in ZSTEPS:
+        pl.semaphore_signal(barrier, inc=1, device_id=along(step)[1], device_id_type=MESH)
+    for steps in PSTEPS:
+        pl.semaphore_signal(barrier, inc=1, device_id=across(steps)[1], device_id_type=MESH)
+    for where in (after, before):
+        pl.semaphore_signal(barrier, inc=1, device_id=where, device_id_type=MESH)
+    loads = [keep(density, dens, own.at[0]), keep(margin, marg.at[pl.ds(2, 24)], own.at[1])]
+    pl.semaphore_wait(barrier, len(ZSTEPS) + len(PSTEPS) + 2)
+
+    halos = [
+        send(margin.at[pl.ds(22, 2)], marg.at[pl.ds(0, 2)], hs.at[0], hr.at[0], after),
+        send(margin.at[pl.ds(0, 2)], marg.at[pl.ds(26, 2)], hs.at[1], hr.at[1], before),
     ]
-    barrier = pltpu.get_barrier_semaphore()
-    for step in zsteps:
-        pl.semaphore_signal(barrier, inc=1, device_id=along(step)[1], device_id_type=MESH)
-    for steps in psteps:
-        pl.semaphore_signal(barrier, inc=1, device_id=across(*steps)[1], device_id_type=MESH)
-    pl.semaphore_wait(barrier, len(zsteps) + len(psteps))
-    copies = []
-    for number in range(len(psteps)):
-        if number < len(zsteps):
-            to, where = along(zsteps[number])
-            copies.append(
-                pltpu.make_async_remote_copy(
-                    src_ref=zsend.at[to], dst_ref=zrecv.at[z], send_sem=zs.at[number], recv_sem=zr.at[number],
-                    device_id=where, device_id_type=MESH,
-                )
+    first_z, first_p = [], []
+    for number in range(len(PSTEPS)):
+        if number < len(ZSTEPS):
+            to, where = along(ZSTEPS[number])
+            first_z.append(send(rows(held, to, CAP), rows(zgot, z, CAP), zs.at[number], zr.at[number], where))
+        to, where = across(PSTEPS[number])
+        first_p.append(send(rows(results, to, 16), rows(pgot, here, 16), ps.at[number], pr.at[number], where))
+    own_z = keep(rows(held, z, CAP), rows(zgot, z, CAP), own.at[2])
+    own_p = keep(rows(results, here, 16), rows(pgot, here, 16), own.at[3])
+
+    def clear(atom, carry):
+        even[atom] = jnp.zeros((BF, WIDE), jnp.bfloat16)
+        odd[atom] = jnp.zeros((BF, WIDE), jnp.bfloat16)
+        return carry
+
+    lax.fori_loop(0, 28, clear, 0)
+    for copy in loads + halos:
+        copy.wait()
+
+    def widen(atom, carry):
+        for block in range(5):
+            piece = marg[atom, block]
+            even[atom, :, (block + 2) * BF : (block + 3) * BF] = piece
+            odd[atom, :, (block + 1) * BF : (block + 2) * BF] = piece
+        return carry
+
+    lax.fori_loop(0, 28, widen, 0)
+
+    def multiply(atom, carry):
+        total = jnp.zeros((BF, 384), jnp.float32)
+        for middle in range(5):
+            wide = even if middle % 2 == 0 else odd
+            start = (4 - middle) // 2 * LANES
+            total = total + jnp.dot(
+                dens[atom, middle], wide[atom + middle, :, start : start + 384], preferred_element_type=jnp.float32
             )
-            copies[-1].start()
-        to, where = across(*psteps[number])
-        copies.append(
-            pltpu.make_async_remote_copy(
-                src_ref=psend.at[to], dst_ref=precv.at[here], send_sem=ps.at[number], recv_sem=pr.at[number],
-                device_id=where, device_id_type=MESH,
-            )
-        )
-        copies[-1].start()
-    mine = [
-        pltpu.make_async_copy(zsend.at[z], zrecv.at[z], own.at[0]),
-        pltpu.make_async_copy(psend.at[here], precv.at[here], own.at[1]),
-    ]
-    for copy in mine:
-        copy.start()
-    for copy in mine + copies:
+        product[atom] = total.astype(jnp.bfloat16)
+        return carry
+
+    lax.fori_loop(0, 24, multiply, 0)
+
+    for copy in first_z:
         copy.wait()
-
-
-def exchange(zsend, psend, number):
+    own_z.wait()
+
+    def gather_owner(to):
+        def body(step, carry):
+            for inner in range(8):
+                spot = to * 16 + step * 8 + inner
+                pput[spot] = zgot[inverse[spot]]
+            return carry
+
+        lax.fori_loop(0, 2, body, 0)
+
+    def owner(number):
+        to, where = across(PSTEPS[number])
+        return send(rows(pput, to, 16), rows(arrived, here, 16), ps2.at[number], pr2.at[number], where)
+
+    second = []
+    gather_owner(across(PSTEPS[0])[0])
+    for number in range(1, len(PSTEPS)):
+        gather_owner(across(PSTEPS[number])[0])
+        second.append(owner(number - 1))
+    gather_owner(here)
+    second.append(owner(len(PSTEPS) - 1))
+
+    for copy in first_p:
+        copy.wait()
+    own_p.wait()
+
+    def gather_holder(to):
+        def body(step, carry):
+            for inner in range(8):
+                spot = to * CAP + step * 8 + inner
+                zput[spot] = pgot[routes[spot]]
+            return carry
+
+        lax.fori_loop(0, CAP // 8, body, 0)
+
+    def holder(number):
+        to, where = along(ZSTEPS[number])
+        return send(rows(zput, to, CAP), rows(back, z, CAP), zs2.at[number], zr2.at[number], where)
+
+    gather_holder(along(ZSTEPS[0])[0])
+    for number in range(1, len(ZSTEPS)):
+        gather_holder(along(ZSTEPS[number])[0])
+        second.append(holder(number - 1))
+    gather_holder(z)
+    second.append(holder(len(ZSTEPS) - 1))
+    second.append(keep(rows(pput, here, 16), rows(arrived, here, 16), own.at[4]))
+    second.append(keep(rows(zput, z, CAP), rows(back, z, CAP), own.at[5]))
+    for copy in second:
+        copy.wait()
+
+
+def exchanged(inverse, routes, held, results, density, margin):
     hbm = pl.BlockSpec(memory_space=pl.ANY)
+    dma = pltpu.SemaphoreType.DMA
     return pl.pallas_call(
         exchange_kernel,
         out_shape=(
-            jax.ShapeDtypeStruct((ZS, CAP * ROWS, LANES), jnp.bfloat16),
-            jax.ShapeDtypeStruct((PLANE, 16 * ROWS, LANES), jnp.bfloat16),
+            BLOCKS,
+            jax.ShapeDtypeStruct((HELD, ROWS, LANES), jnp.bfloat16),
+            jax.ShapeDtypeStruct((24, BF, 384), jnp.bfloat16),
         ),
-        in_specs=[hbm, hbm],
-        out_specs=(hbm, hbm),
+        in_specs=[SMEM, SMEM, hbm, hbm, hbm, hbm],
+        out_specs=(hbm, hbm, VM),
         scratch_shapes=[
-            pltpu.SemaphoreType.DMA((7,)),
-            pltpu.SemaphoreType.DMA((7,)),
-            pltpu.SemaphoreType.DMA((31,)),
-            pltpu.SemaphoreType.DMA((31,)),
-            pltpu.SemaphoreType.DMA((2,)),
+            pltpu.VMEM((HELD, ROWS, LANES), jnp.bfloat16),
+            pltpu.VMEM((SLOTS_ALL, ROWS, LANES), jnp.bfloat16),
+            pltpu.VMEM((HELD, ROWS, LANES), jnp.bfloat16),
+            pltpu.VMEM((SLOTS_ALL, ROWS, LANES), jnp.bfloat16),
+            pltpu.VMEM((24, 5, BF, BF), jnp.bfloat16),
+            pltpu.VMEM((28, 5, BF, BF), jnp.bfloat16),
+            pltpu.VMEM((28, BF, WIDE), jnp.bfloat16),
+            pltpu.VMEM((28, BF, WIDE), jnp.bfloat16),
+            dma((7,)), dma((7,)), dma((31,)), dma((31,)),
+            dma((7,)), dma((7,)), dma((31,)), dma((31,)),
+            dma((2,)), dma((2,)), dma((6,)),
         ],
-        compiler_params=params(collective_id=number, has_side_effects=True),
+        compiler_params=params(collective_id=0, has_side_effects=True),
         name="exchange",
-    )(zsend, psend)
-
-
-def swap_kernel(spot, held, results, out, back):
-    def body(step, carry):
-        for inner in range(8):
-            item = step * 8 + inner
-            where = spot[item]
-            out[where] = held[item]
-            back[item] = results[jnp.minimum(where, SLOTS_ALL - 1)]
-        return carry
-
-    lax.fori_loop(0, HELD // 8, body, 0)
+    )(inverse, routes, held, results, density, margin)
 
 
 def matrix_kernel(label, basis, potential, out, scaled, table):
@@ -202,7 +285,7 @@
         lax.fori_loop(0, SLOTS_ALL // 16, body, 0)
 
 
-def grid_kernel(label, blocks, basis, out, table, weights):
+def grid_kernel(label, place, blocks, basis, back, product, out, ks, margins, table, weights):
     task = pl.program_id(0)
 
     @pl.when(task == 0)
@@ -242,6 +325,13 @@
         phi = basis[0, :, columns]
         weighted = jnp.dot(weights[...], phi, preferred_element_type=jnp.float32)
         out[0, :, columns] = jnp.sum(phi.astype(jnp.float32) * weighted, axis=0, keepdims=True)
+    for pair in range(15):
+        block = back[place[task * 15 + pair]]
+        ks[pair, 0:ROWS] = block[:, 0:BF]
+        ks[pair, ROWS:BF] = block[:, BF:LANES]
+    for atom in range(3):
+        for offset in range(5):
+            margins[atom * 5 + offset] = product[atom, :, offset * BF : (offset + 1) * BF]
 
 
 def params(**more):
@@ -267,32 +357,6 @@
         cost_estimate=pl.CostEstimate(flops=0, bytes_accessed=6 << 20, transcendentals=0),
         name="pack",
     )(places, flat)
-
-
-def unpacked(places, blocks):
-    return pl.pallas_call(
-        unpack_kernel,
-        out_shape=jax.ShapeDtypeStruct((PAIRS, BF, BF), jnp.bfloat16),
-        in_specs=[SMEM, VM],
-        out_specs=VM,
-        compiler_params=params(),
-        cost_estimate=pl.CostEstimate(flops=0, bytes_accessed=6 << 20, transcendentals=0),
-        name="unpack",
-    )(places, blocks)
-
-
-def swapped(spot, held, results):
-    return pl.pallas_call(
-        swap_kernel,
-        out_shape=(
-            jax.ShapeDtypeStruct((SLOTS_ALL + 16, ROWS, LANES), jnp.bfloat16),
-            jax.ShapeDtypeStruct((HELD, ROWS, LANES), jnp.bfloat16),
-        ),
-        in_specs=[SMEM, VM, VM],
-        out_specs=(VM, VM),
-        compiler_params=params(),
-        name="swap",
-    )(spot, held, results)
 
 
 def by_plane(values):
@@ -344,8 +408,16 @@
     labels = jnp.where(tags[:, 0] < 0, -1, tags[:, 0] * 64 + tags[:, 1] * 8 + tags[:, 2]).reshape(SLOTS_ALL)
     here = row // 2 * 2 + col % 2
     targets = lax.dynamic_index_in_dim(by_plane(notes[:, 8 : 8 + CAP]).reshape(PLANE, ZS, CAP), here, 0, keepdims=False)
-    number = jnp.arange(HELD, dtype=jnp.int32).reshape(ZS, CAP)
-    routes = jnp.where(targets < 0, SLOTS_ALL + number % 16, targets // 2 * 16 + number // CAP * 2 + targets % 2).reshape(HELD)
+    number = jnp.arange(HELD, dtype=jnp.int32)
+    targets = targets.reshape(HELD)
+    routes = targets // 2 * 16 + number // CAP * 2 + targets % 2
+    inverse = jnp.sum(
+        jnp.where(
+            (jnp.arange(SLOTS_ALL, dtype=jnp.int32)[:, None] == routes[None, :]) & (targets >= 0)[None, :], number[None, :], 0
+        ),
+        axis=1,
+    )
+    routes = jnp.where(targets < 0, 0, routes)
 
     phi = basis_values.reshape(TASKS, BASIS, POINTS)
     results = pl.pallas_call(
@@ -367,39 +439,54 @@
         name="matrices",
     )(labels, phi, box_potential)
 
-    margin_product = margin_of(density, margin)
-    results, margin_product = lax.optimization_barrier((results, margin_product))
-
-    def fast(results, held, flat, places, spots, routes):
-        got_z, got_p = exchange(held.reshape(ZS + 1, CAP * ROWS, LANES), results.reshape(PLANE, 16 * ROWS, LANES), 0)
-        out, back = swapped(routes, got_z.reshape(HELD, ROWS, LANES), got_p.reshape(BLOCKS.shape))
-        back, arrived = exchange(back.reshape(ZS, CAP * ROWS, LANES), out.reshape(PLANE + 1, 16 * ROWS, LANES), 1)
-        return arrived.reshape(BLOCKS.shape), unpacked(spots, back.reshape(HELD, ROWS, LANES))
-
-    def dense(results, held, flat, places, spots, routes):
-        outgoing = packed(places, flat, SLOTS_ALL)
+    def fast(results, held, density, margin, places, routes, inverse):
+        return exchanged(inverse, routes, held, results, density, margin)
+
+    def dense(results, held, density, margin, places, routes, inverse):
+        outgoing = packed(places, density.reshape(PAIRS, BF, BF), SLOTS_ALL)
         arrived = by_plane(lax.all_to_all(outgoing.reshape(PEERS, 64, LANES), ALL, 0, 0, tiled=True))
         returned = lax.all_to_all(by_mesh(results.reshape(PEERS, 64, LANES)), ALL, 0, 0, tiled=True)
-        return arrived.reshape(BLOCKS.shape), unpacked(places, returned.reshape(BLOCKS.shape))
-
-    arrived, ks_blocks = lax.cond(over, dense, fast, results, held, flat, places, spots, routes)
-
-    grid_rows = pl.pallas_call(
+        back = returned.reshape(BLOCKS.shape)[places]
+        wide = margin_of(density, margin).transpose(0, 2, 1, 3).reshape(atoms_here, BF, offsets * BF)
+        return (
+            arrived.reshape(BLOCKS.shape),
+            jnp.pad(back, ((0, HELD - PAIRS), (0, 0), (0, 0))),
+            jnp.pad(wide, ((0, 0), (0, 0), (0, BF))),
+        )
+
+    arrived, back, product = lax.cond(over, dense, fast, results, held, density, margin, places, routes, inverse)
+    pickup = jnp.where(over, jnp.arange(PAIRS, dtype=jnp.int32), spots)
+
+    grid_rows, ks_blocks, margin_product = pl.pallas_call(
         grid_kernel,
-        out_shape=jax.ShapeDtypeStruct((TASKS, 1, POINTS), jnp.float32),
+        out_shape=(
+            jax.ShapeDtypeStruct((TASKS, 1, POINTS), jnp.float32),
+            jax.ShapeDtypeStruct((PAIRS, BF, BF), jnp.bfloat16),
+            jax.ShapeDtypeStruct((PAIRS, BF, BF), jnp.bfloat16),
+        ),
         grid=(TASKS,),
-        in_specs=[SMEM, whole(BLOCKS.shape), pl.BlockSpec((1, BASIS, POINTS), lambda t: (t, 0, 0))],
-        out_specs=pl.BlockSpec((1, 1, POINTS), lambda t: (t, 0, 0)),
+        in_specs=[
+            SMEM,
+            SMEM,
+            whole(BLOCKS.shape),
+            pl.BlockSpec((1, BASIS, POINTS), lambda t: (t, 0, 0)),
+            whole((HELD, ROWS, LANES)),
+            pl.BlockSpec((3, BF, 384), lambda t: (t, 0, 0)),
+        ],
+        out_specs=(
+            pl.BlockSpec((1, 1, POINTS), lambda t: (t, 0, 0)),
+            pl.BlockSpec((15, BF, BF), lambda t: (t, 0, 0)),
+            pl.BlockSpec((15, BF, BF), lambda t: (t, 0, 0)),
+        ),
         scratch_shapes=[
             pltpu.VMEM((SLOTS_ALL + 1, ROWS, LANES), jnp.float32),
             pltpu.VMEM((BASIS, BASIS), jnp.bfloat16),
         ],
         compiler_params=params(),
-        cost_estimate=pl.CostEstimate(flops=2 * TASKS * BASIS * BASIS * POINTS, bytes_accessed=14 << 20, transcendentals=0),
         name="collocate",
-    )(labels, arrived, phi)
+    )(labels, pickup, arrived, phi, back, product)
     density_grid = grid_rows.reshape(32, 1, 256)
-    return density_grid, ks_blocks.reshape(atoms_here, offsets, BF, BF), margin_product
+    return density_grid, ks_blocks.reshape(atoms_here, offsets, BF, BF), margin_product.reshape(atoms_here, offsets, BF, BF)
 
 
 def solution(mesh):

time: 210 us -> 194 us (0.924)
  Pallas kernels: 159 us -> 147 us
  waiting for transfers between devices: 3.9 us -> 15 us
  matrix products: 6.91 us -> 0 us
  local copies, waits for them, and re-layouts: 13.2 us -> 7.27 us
  starting transfers between devices: 18.7 us -> 15.6 us
    all_to_all x1, waiting for transfers between devices: 0.01 us -> 15 us  [local(): lax.all_to_all(sent, ALL, 0, 0, tiled=True).reshape(PEERS, LANES + 256)]
    pallas_call x5 -> x2, Pallas kernels: 142 us -> 131 us  [the longest x1 115 us: exchanged(): pl.pallas_call(exchange_kernel, out_shape=(BLOCKS, jax.ShapeDtypeStruct((...]
    dot_general x5 -> x0, matrix products: 6.91 us -> none  [margin_of(): jnp.einsum('amik,amkj->aij', left_blocks, right_blocks, preferred_element...]
    unnamed x22 -> x13, local copies, waits for them, and re-layouts: 8.39 us -> 1.6 us
    ppermute x2 -> x0, starting transfers between devices: 5.32 us -> none  [the longest x1 3.09 us: padded(): before = lax.ppermute(last, axis, up)]
    ppermute x2 -> x0, waiting for transfers between devices: 3.9 us -> none  [the longest x1 3.89 us: padded(): after = lax.ppermute(first, axis, down)]
    all_to_all x1, starting transfers between devices: 13.4 us -> 15.6 us  [local(): lax.all_to_all(sent, ALL, 0, 0, tiled=True).reshape(PEERS, LANES + 256)]
  transfers between devices with their start and end apart: 3 -> 1, of which waited for: 1 -> 1; matrix products, arithmetic and copies ran while one was open for 6% -> 0% of each run, Pallas kernels for 2% -> 2%
where the time goes in v3:
time: 194 us; the launch traced here: 191 us
  Pallas kernels  147 us (76%)
  starting transfers between devices  15.6 us (8%)
  waiting for transfers between devices  15 us (8%)
  local copies, waits for them, and re-layouts  7.27 us (4%)
  other arithmetic  4.2 us (2%)
  between operations  2.39 us (1%)
    pallas_call x1, Pallas kernels, exchanged(): pl.pallas_call(exchange_kernel, out_shape=(BLOCKS, jax.ShapeDtypeStruct((...  115 us
    pallas_call x1, Pallas kernels, local(): pl.pallas_call(grid_kernel, out_shape=(jax.ShapeDtypeStruct((TASKS, 1, PO...  15.8 us
    all_to_all x1, starting transfers between devices, local(): lax.all_to_all(sent, ALL, 0, 0, tiled=True).reshape(PEERS, LANES + 256)  15.6 us
    all_to_all x1, waiting for transfers between devices, local(): lax.all_to_all(sent, ALL, 0, 0, tiled=True).reshape(PEERS, LANES + 256)  15 us
    pallas_call x1, Pallas kernels, local(): pl.pallas_call(matrix_kernel, out_shape=BLOCKS, grid=(TASKS,), in_specs=[...  12.2 us
  transfers between devices with their start and end apart: 1, of which 1 were waited for; matrix products, arithmetic and copies ran while one was open for 0% of the time, Pallas kernels for 2%

profile of v3, /device:TPU:1, one launch (start us, length us, event | category | flops | bytes accessed | tf_op | source)
XLA Modules:
  0.0 191.4 jit_solution(11116774456490416265)
XLA Ops:
  0.6 0.0 copy-start
  0.7 0.1 pad.31.clone
  0.7 0.8 fusion.121
  1.5 0.1 copy.66
  1.6 0.1 stack.49
  1.7 0.1 copy.67
  1.8 0.1 stack.50
  1.9 0.8 copy.64
  2.6 0.1 reshape.448
  2.7 0.2 convert_reduce_fusion.1
  3.0 0.2 convert_reduce_fusion
  3.1 0.6 fusion.122
  4.4 0.1 pad.29.clone
  4.5 0.1 select_reduce_fusion.2
  4.6 0.1 sub.50
  4.7 0.8 copy.65
  5.5 0.1 stack.48
  5.6 0.1 iota_compare_fusion.1
  5.7 0.1 select_reduce_fusion.1
  5.9 0.0 copy-done
  5.9 0.0 copy-start.2
  5.9 0.3 sub.45
  6.3 0.1 copy.68
  6.4 0.1 copy.69
  6.6 0.1 add_convert_fusion
  6.8 1.0 reshape.452
  7.8 0.0 copy-done.6
  7.8 15.6 %all-to-all-start.2 = ((f32[256,1,384]{2,1,0:T(1,128)}), f32[256,1,384]{2,1,0:T(1,128)S(1)}, u32[]{:S(2)}, u32[]{:S(2)}) async-start(f32[256,1,384]{2,1,0:T(1,128)} %reshape.452), calls=%async_computation.2 | async-start | bytes 786432 | tf_op jit(solution)/shard_map/all_to_all | solution.py:402
  23.5 0.0 copy-start.7
  23.5 3.7 %pack.3 = bf16[288,32,128]{2,1,0:T(8,128)(2,1)} custom-call(s32[120]{0:T(128)} %copy-done.6, bf16[120,64,64]{2,1,0:T(8,128)(2,1)S(1)} %bitcast.127), custom_call_target="tpu_custom_call" | custom-call | bytes 6291456 | tf_op jit(solution)/shard_map/pack/pallas_call | solution.py:351
  27.2 15.0 %all-to-all-done.2 = f32[256,1,384]{2,1,0:T(1,128)S(1)} async-done(((f32[256,1,384]{2,1,0:T(1,128)}), f32[256,1,384]{2,1,0:T(1,128)S(1)}, u32[]{:S(2)}, u32[]{:S(2)}) %all-to-all-start.2) | async-done | bytes 393248 | tf_op jit(solution)/shard_map/all_to_all | solution.py:402
  42.3 0.7 slice_reduce_fusion
  43.7 0.5 broadcast_select_fusion.place
  44.2 0.1 slice.169
  44.3 0.3 copy.70
  44.6 0.2 reshape_reshape.6
  44.8 0.1 copy.71
  45.0 0.7 select_n.176.label
  45.7 0.6 constant_dynamic-slice_fusion
  46.4 12.2 %matrices.1 = bf16[512,32,128]{2,1,0:T(8,128)(2,1)} custom-call(s32[512]{0:T(512)} %select_n.176.label, bf16[8,512,1024]{2,1,0:T(8,128)(2,1)} %bitcast.132, f32[8,1,1024]{2,1,0:T(1,128)} %bitcast.145), custom_call_target="tpu_custom_call" | custom-call | flops 4294967296 | bytes 14680064 | tf_op jit(solution)/shard_map/matrices/pallas_call | solution.py:423
  58.7 116.7 %conditional.1 = ((bf16[512,32,128]{2,1,0:T(8,128)(2,1)}, bf16[256,32,128]{2,1,0:T(8,128)(2,1)}, bf16[24,64,384]{2,1,0:T(8,128)(2,1)S(1)})) conditional(s32[]{:T(128)} %convert_element_type.28, (s32[1,8,32]{2,1,0:T(8,128)S(1)}, (), s32[]{:T(128)}, s32[1,256]{1,0:T(1,128)S(1)}, s32[512,256]{1,0:T(8,128)S(1)}, /*index=5*/s32[512,256]{1,0:T(8,128)S(1)}, ...), branch_computations={%region_6.8_spmd, %region_8.9_spmd} | conditional | flops 250873184 | bytes 111401096 | solution.py:457
  58.7 0.1 reshape.479
  58.8 0.8 select_reduce_fusion.inverse
  59.6 0.1 reshape.480
  59.7 0.6 fusion.111.routes
  60.2 114.9 %exchange.1 = (bf16[512,32,128]{2,1,0:T(8,128)(2,1)}, bf16[256,32,128]{2,1,0:T(8,128)(2,1)}, bf16[24,64,384]{2,1,0:T(8,128)(2,1)S(1)}) custom-call(s32[512]{0:T(512)} %select_reduce_fusion.inverse, s32[256]{0:T(256)} %fusion.111.routes, bf16[288,32,128]{2,1,0:T(8,128)(2,1)} %get-tuple-element.203.held, bf16[512,32,128]{2,1,0:T(8,128)(2,1)} %get-tuple-element.204.results, ...), custom_call_target="tpu_custom_call" | custom-call | tf_op jit(solution)/shard_map/cond/branch_0_fun/exchange/pallas_call | solution.py:233
  175.4 0.0 copy-start.1
  175.4 15.8 %collocate.1 = (f32[8,1,1024]{2,1,0:T(1,128)}, bf16[120,64,64]{2,1,0:T(8,128)(2,1)}, bf16[120,64,64]{2,1,0:T(8,128)(2,1)}) custom-call(s32[512]{0:T(512)} %select_n.176.label, s32[120]{0:T(128)} %broadcast_select_fusion.place, bf16[512,32,128]{2,1,0:T(8,128)(2,1)} %get-tuple-element.220.blocks, bf16[8,512,1024]{2,1,0:T(8,128)(2,1)} %bitcast.133, ...), custom_call_target="tpu_custom_call" | custom-call | tf_op jit(solution)/shard_map/collocate/pallas_call | solution.py:460
  (26 shorter events, 0.4 us)
Async XLA Ops:
  0.6 5.2 %copy-start = (f32[1,32,256]{2,1,0:T(8,128)S(1)}, f32[1,32,256]{2,1,0:T(8,128)}, u32[]{:S(2)}) copy-start(f32[1,32,256]{2,1,0:T(8,128)} %param.11) | copy-start | bytes 98308
  3.8 4.0 %copy-start.6 = (s32[120]{0:T(128)}, s32[120]{0:T(128)S(1)}, u32[]{:S(2)}) copy-start(s32[120]{0:T(128)S(1)} %get-tuple-element.303.place) | copy-start | bytes 1444
  5.9 17.6 %copy-start.2 = (bf16[24,5,64,64]{3,2,1,0:T(8,128)(2,1)S(1)}, bf16[24,5,64,64]{3,2,1,0:T(8,128)(2,1)}, u32[]{:S(2)}) copy-start(bf16[24,5,64,64]{3,2,1,0:T(8,128)(2,1)} %param.9) | copy-start | bytes 2949124
  7.8 34.4 %all-to-all-start.2 = ((f32[256,1,384]{2,1,0:T(1,128)}), f32[256,1,384]{2,1,0:T(1,128)S(1)}, u32[]{:S(2)}, u32[]{:S(2)}) async-start(f32[256,1,384]{2,1,0:T(1,128)} %reshape.452), calls=%async_computation.2 | async-start | bytes 786432 | tf_op jit(solution)/shard_map/all_to_all | solution.py:402
  23.5 20.2 %copy-start.7 = (s32[120]{0:T(128)S(1)}, s32[120]{0:T(128)}, u32[]{:S(2)}) copy-start(s32[120]{0:T(128)} %copy-done.6) | copy-start | bytes 1444
  175.4 15.8 %copy-start.1 = (f32[1,32,256]{2,1,0:T(8,128)S(1)}, f32[1,32,256]{2,1,0:T(8,128)}, u32[]{:S(2)}) copy-start(f32[1,32,256]{2,1,0:T(8,128)} %param.11) | copy-start | bytes 98308

commit v4 on v3

--- a/solution.py
+++ b/solution.py
@@ -20,7 +20,7 @@
 ALL = ("row", "col")
 ZS = 8
 PLANE = 32
-CAP = 32
+CAP = 28
 HELD = ZS * CAP
 MESH = pl.DeviceIdType.MESH
 VMEM_LIMIT = 56 * 1024 * 1024
@@ -204,12 +204,12 @@
 
     def gather_holder(to):
         def body(step, carry):
-            for inner in range(8):
-                spot = to * CAP + step * 8 + inner
+            for inner in range(4):
+                spot = to * CAP + step * 4 + inner
                 zput[spot] = pgot[routes[spot]]
             return carry
 
-        lax.fori_loop(0, CAP // 8, body, 0)
+        lax.fori_loop(0, CAP // 4, body, 0)
 
     def holder(number):
         to, where = along(ZSTEPS[number])
@@ -257,6 +257,98 @@
     )(inverse, routes, held, results, density, margin)
 
 
+def notice_kernel(
+    which, table, potential, density, got, pencil, held, zgot, other, zs, zr, ps, pr, qs, qr, us, ur, own
+):
+    row, col = lax.axis_index("row"), lax.axis_index("col")
+    y, x, high = row // 8, lax.rem(row // 2, 4), lax.rem(row, 2)
+    low, core = col // 2, lax.rem(col, 2)
+    z = high * 4 + low
+    here = (y * 4 + x) * 2 + core
+    flipped = y * 8 + x * 2 + (1 - high)
+
+    def along(step):
+        to = lax.rem(z + step, ZS)
+        return to, (y * 8 + x * 2 + to // 4, lax.rem(to, 4) * 2 + core)
+
+    def across(steps):
+        dy, dx, dc = steps
+        to_y, to_x, to_c = lax.rem(y + dy, 4), lax.rem(x + dx, 4), lax.rem(core + dc, 2)
+        return (to_y * 4 + to_x) * 2 + to_c, (to_y * 8 + to_x * 2 + high, low * 2 + to_c)
+
+    def send(source, target, sent, received, where):
+        copy = pltpu.make_async_remote_copy(
+            src_ref=source, dst_ref=target, send_sem=sent, recv_sem=received, device_id=where, device_id_type=MESH
+        )
+        copy.start()
+        return copy
+
+    def keep(source, target, semaphore):
+        copy = pltpu.make_async_copy(source, target, semaphore)
+        copy.start()
+        return copy
+
+    barrier = pltpu.get_barrier_semaphore()
+    for step in ZSTEPS:
+        pl.semaphore_signal(barrier, inc=1, device_id=along(step)[1], device_id_type=MESH)
+    for steps in PSTEPS:
+        pl.semaphore_signal(barrier, inc=1, device_id=across(steps)[1], device_id_type=MESH)
+    pl.semaphore_wait(barrier, len(ZSTEPS) + len(PSTEPS))
+
+    first = [send(potential, other, zs.at[7], zr.at[7], along(4)[1])]
+    for number in range(len(ZSTEPS)):
+        to, where = along(ZSTEPS[number])
+        first.append(send(table.at[to], zgot.at[z], zs.at[number], zr.at[number], where))
+    first.append(keep(table.at[z], zgot.at[z], own.at[0]))
+
+    def pack(step, carry):
+        for inner in range(8):
+            spot = step * 8 + inner
+            block = density[which[spot]]
+            held[spot, :, 0:BF] = block[0:ROWS]
+            held[spot, :, BF:LANES] = block[ROWS:BF]
+        return carry
+
+    lax.fori_loop(0, HELD // 8, pack, 0)
+    for copy in first:
+        copy.wait()
+
+    second, line = [], 0
+    for number in range(len(PSTEPS)):
+        to, where = across(PSTEPS[number])
+        second.append(send(zgot.at[:, to], got.at[here], ps.at[number], pr.at[number], where))
+        if PSTEPS[number][2] == 0:
+            second.append(send(potential.at[where[0]], pencil.at[row], qs.at[line], qr.at[line], where))
+            second.append(send(other.at[where[0]], pencil.at[flipped], us.at[line], ur.at[line], where))
+            line += 1
+    second.append(keep(zgot.at[:, here], got.at[here], own.at[1]))
+    second.append(keep(potential.at[row], pencil.at[row], own.at[2]))
+    second.append(keep(other.at[row], pencil.at[flipped], own.at[3]))
+    for copy in second:
+        copy.wait()
+
+
+def noticed(which, table, potential, flat):
+    dma = pltpu.SemaphoreType.DMA
+    return pl.pallas_call(
+        notice_kernel,
+        out_shape=(
+            jax.ShapeDtypeStruct((PLANE, ZS, 1, LANES), jnp.int32),
+            jax.ShapeDtypeStruct((32, 1, 256), jnp.float32),
+            jax.ShapeDtypeStruct((HELD, ROWS, LANES), jnp.bfloat16),
+        ),
+        in_specs=[SMEM, VM, VM, VM],
+        out_specs=(VM, VM, VM),
+        scratch_shapes=[
+            pltpu.VMEM((ZS, PLANE, 1, LANES), jnp.int32),
+            pltpu.VMEM((32, 1, 256), jnp.float32),
+            dma((8,)), dma((8,)), dma((31,)), dma((31,)), dma((15,)), dma((15,)), dma((15,)), dma((15,)), dma((4,)),
+        ],
+        compiler_params=params(collective_id=1, has_side_effects=True),
+        name="notices",
+    )(which, table, potential, flat)
+
+
 def matrix_kernel(label, basis, potential, out, scaled, table):
     task = pl.program_id(0)
     phi = basis[0]
@@ -375,39 +467,45 @@
     owners = pair_owner.reshape(PAIRS)
     planes = (owners // 8) % 2 * 4 + owners % 8 // 2
     inside = owners // 16 * 2 + owners % 2
-    before = jnp.arange(PAIRS)[:, None] > jnp.arange(PAIRS)[None, :]
+    order = jnp.arange(PAIRS, dtype=jnp.int32)
+    before = order[:, None] > order[None, :]
     ranks = jnp.sum(((owners[:, None] == owners[None, :]) & before).astype(jnp.int32), axis=1)
     turns = jnp.sum(((planes[:, None] == planes[None, :]) & before).astype(jnp.int32), axis=1)
     places = owners * 2 + ranks
     spots = jnp.where(turns < CAP, planes * CAP + turns, HELD)
     flat = density.reshape(PAIRS, BF, BF)
-    held = packed(spots, flat, HELD + CAP)
-
-    fields = jnp.stack(
-        [pair_box.reshape(PAIRS), pair_slots[..., 0].reshape(PAIRS), pair_slots[..., 1].reshape(PAIRS)], axis=0
+    which = jnp.sum(
+        jnp.where(jnp.arange(HELD, dtype=jnp.int32)[:, None] == spots[None, :], order[None, :], 0), axis=1
     )
-    chosen = jnp.arange(SLOTS_ALL, dtype=jnp.int32)[None, :, None] == places[None, None, :]
-    tags = jnp.sum(jnp.where(chosen, fields[:, None, :] + 1, 0), axis=2) - 1
-    tags = tags.reshape(3, PEERS, 2).transpose(1, 0, 2).reshape(PEERS, 6)
-    listed = jnp.arange(HELD, dtype=jnp.int32)[:, None] == spots[None, :]
-    targets = jnp.sum(jnp.where(listed, (inside * 2 + ranks)[None, :] + 1, 0), axis=1) - 1
-    targets = jnp.broadcast_to(targets.reshape(1, ZS, 1, CAP), (16, ZS, 2, CAP)).reshape(PEERS, CAP)
     over = jnp.max(turns) >= CAP
-    rows = jnp.broadcast_to(potential[0][:, None, :], (32, 8, 256)).reshape(PEERS, 256)
-    notes = jnp.concatenate(
-        [tags, jnp.broadcast_to(over.astype(jnp.int32), (PEERS, 2)), targets, jnp.zeros((PEERS, LANES - 8 - CAP), jnp.int32)],
-        axis=1,
-    ).astype(jnp.float32)
-    sent = jnp.concatenate([notes, rows], axis=1).reshape(PEERS, 1, LANES + 256)
-    got = lax.all_to_all(sent, ALL, 0, 0, tiled=True).reshape(PEERS, LANES + 256)
-    notes = got[:, :LANES].astype(jnp.int32)
-    pencil = lax.dynamic_index_in_dim(got[:, LANES:].reshape(32, 8, 256), col, 1, keepdims=False)
+    lanes = jnp.arange(LANES, dtype=jnp.int32)[None, :]
+    peers = jnp.arange(PEERS, dtype=jnp.int32)[:, None]
+
+    def column(values):
+        return values.reshape(PAIRS, 1)
+
+    box, one, two = column(pair_box), column(pair_slots[..., 0]), column(pair_slots[..., 1])
+    field = jnp.where(lanes < 2, box, jnp.where(lanes < 4, one, two)) + 1
+    to_owner = jnp.where((lanes < 6) & (lanes % 2 == column(ranks)), field, 0)
+    to_plane = jnp.where(lanes - 8 == column(turns), column(inside * 2 + ranks) + 1, 0)
+    at_owner = peers == (planes * PLANE + inside)[None, :]
+    at_plane = peers // PLANE == planes[None, :]
+
+    def listed(chosen, values):
+        return jnp.dot(chosen.astype(jnp.bfloat16), values.astype(jnp.bfloat16), preferred_element_type=jnp.float32)
+
+    table = (listed(at_owner, to_owner) + listed(at_plane, to_plane)).astype(jnp.int32) - 1
+    table = jnp.where(lanes == 6, over.astype(jnp.int32), table)
+    got, pencil, held = noticed(
+        which, table.reshape(ZS, PLANE, 1, LANES), potential.reshape(32, 1, 256), flat
+    )
     box_potential = pencil.reshape(TASKS, 1, POINTS)
-    over = jnp.max(notes[:, 6]) > 0
-    tags = by_plane(notes[:, :6]).reshape(PEERS, 3, 2)
-    labels = jnp.where(tags[:, 0] < 0, -1, tags[:, 0] * 64 + tags[:, 1] * 8 + tags[:, 2]).reshape(SLOTS_ALL)
+    got = got.reshape(PEERS, LANES)
+    over = jnp.max(got[:, 6]) > 0
+    tags = got[:, 0:2] * 64 + got[:, 2:4] * 8 + got[:, 4:6]
+    labels = jnp.where(got[:, 0:2] < 0, -1, tags).reshape(SLOTS_ALL)
     here = row // 2 * 2 + col % 2
-    targets = lax.dynamic_index_in_dim(by_plane(notes[:, 8 : 8 + CAP]).reshape(PLANE, ZS, CAP), here, 0, keepdims=False)
+    targets = lax.dynamic_slice(got, (here * ZS, 8), (ZS, CAP))
     number = jnp.arange(HELD, dtype=jnp.int32)
     targets = targets.reshape(HELD)
     routes = targets // 2 * 16 + number // CAP * 2 + targets % 2

time: 194 us -> 192 us (0.990)
  Pallas kernels: 147 us -> 173 us
  starting transfers between devices: 15.6 us -> 0 us
  waiting for transfers between devices: 15 us -> 0 us
  other arithmetic: 4.2 us -> 6.57 us
    pallas_call x1, Pallas kernels: 3.72 us -> 26.7 us  [noticed(): pl.pallas_call(notice_kernel, out_shape=(jax.ShapeDtypeStruct((PLANE, ZS,...]
    all_to_all x1 -> x0, starting transfers between devices: 15.6 us -> none  [local(): lax.all_to_all(sent, ALL, 0, 0, tiled=True).reshape(PEERS, LANES + 256)]
    all_to_all x1 -> x0, waiting for transfers between devices: 15 us -> none  [local(): lax.all_to_all(sent, ALL, 0, 0, tiled=True).reshape(PEERS, LANES + 256)]
    pallas_call x1, Pallas kernels: 115 us -> 119 us  [exchanged(): pl.pallas_call(exchange_kernel, out_shape=(BLOCKS, jax.ShapeDtypeStruct((...]
  transfers between devices with their start and end apart: 1 -> 0, of which waited for: 1 -> 0; matrix products, arithmetic and copies ran while one was open for 0% -> 0% of each run, Pallas kernels for 2% -> 0%
where the time goes in v4:
time: 192 us; the launch traced here: 189 us
  Pallas kernels  173 us (90%)
  other arithmetic  6.57 us (3%)
  local copies, waits for them, and re-layouts  5.96 us (3%)
  between operations  2.09 us (1%)
    pallas_call x1, Pallas kernels, exchanged(): pl.pallas_call(exchange_kernel, out_shape=(BLOCKS, jax.ShapeDtypeStruct((...  119 us
    pallas_call x1, Pallas kernels, noticed(): pl.pallas_call(notice_kernel, out_shape=(jax.ShapeDtypeStruct((PLANE, ZS,...  26.7 us
    pallas_call x1, Pallas kernels, local(): pl.pallas_call(grid_kernel, out_shape=(jax.ShapeDtypeStruct((TASKS, 1, PO...  15.3 us
    pallas_call x1, Pallas kernels, local(): pl.pallas_call(matrix_kernel, out_shape=BLOCKS, grid=(TASKS,), in_specs=[...  12.4 us

profile of v4, /device:TPU:1, one launch (start us, length us, event | category | flops | bytes accessed | tf_op | source)
XLA Modules:
  0.0 189.3 jit_solution(147588572677685452)
XLA Ops:
  0.7 0.8 fusion.149
  1.5 0.1 copy.42
  1.6 0.1 broadcast_in_dim.134
  1.7 0.1 copy.43
  1.8 0.1 broadcast_in_dim.136
  1.9 0.8 copy.40
  2.7 0.1 reshape.484
  2.8 0.2 convert_reduce_fusion
  3.0 0.2 convert_reduce_fusion.1
  3.2 0.6 fusion.150
  4.5 0.7 select_reduce_fusion.1.which
  5.1 0.8 copy.41
  5.9 0.1 broadcast_in_dim.131
  6.0 1.4 reshape.486.potential
  7.4 0.3 fusion.117
  7.7 0.9 fusion.114
  8.7 26.7 %notices.1 = (s32[32,8,1,128]{3,2,1,0:T(1,128)}, f32[32,1,256]{2,1,0:T(1,128)}, bf16[224,32,128]{2,1,0:T(8,128)(2,1)}) custom-call(s32[224]{0:T(256)} %select_reduce_fusion.1.which, s32[8,32,1,128]{3,2,1,0:T(1,128)} %bitcast.118, f32[32,1,256]{2,1,0:T(1,128)} %reshape.486.potential, bf16[120,64,64]{2,1,0:T(8,128)(2,1)} %bitcast.105), custom_call_target="tpu_custom_call" | custom-call | tf_op jit(solution)/shard_map/notices/pallas_call | solution.py:333
  35.3 1.6 slice_reduce_fusion
  37.6 0.6 broadcast_select_fusion.place
  38.2 0.7 constant_dynamic-slice_fusion
  39.0 1.2 fusion.115
  40.2 0.7 reshape.489.label
  40.9 0.0 copy-start
  40.9 12.4 %matrices.1 = bf16[512,32,128]{2,1,0:T(8,128)(2,1)} custom-call(s32[512]{0:T(512)} %reshape.489.label, bf16[8,512,1024]{2,1,0:T(8,128)(2,1)} %bitcast.110, f32[8,1,1024]{2,1,0:T(1,128)} %bitcast.122), custom_call_target="tpu_custom_call" | custom-call | flops 4294967296 | bytes 14680064 | tf_op jit(solution)/shard_map/matrices/pallas_call | solution.py:521
  53.3 0.0 copy-done
  53.3 120.7 %conditional.1 = ((bf16[512,32,128]{2,1,0:T(8,128)(2,1)}, bf16[224,32,128]{2,1,0:T(8,128)(2,1)}, bf16[24,64,384]{2,1,0:T(8,128)(2,1)S(1)})) conditional(s32[]{:T(128)} %convert_element_type.34, (s32[8,28]{1,0:T(8,128)S(1)}, (), s32[]{:T(128)}, s32[1,224]{1,0:T(1,128)S(1)}, s32[512,224]{1,0:T(8,128)S(1)}, /*index=5*/s32[512,224]{1,0:T(8,128)S(1)}, ...), branch_computations={%region_5.7_spmd, %region_7.8_spmd} | conditional | flops 250873440 | bytes 111139928 | solution.py:555
  53.3 0.1 reshape.511
  53.4 0.8 select_reduce_fusion.inverse
  54.2 0.1 reshape.512
  54.2 0.6 fusion.111.routes
  54.8 118.9 %exchange.1 = (bf16[512,32,128]{2,1,0:T(8,128)(2,1)}, bf16[224,32,128]{2,1,0:T(8,128)(2,1)}, bf16[24,64,384]{2,1,0:T(8,128)(2,1)S(1)}) custom-call(s32[512]{0:T(512)} %select_reduce_fusion.inverse, s32[224]{0:T(256)} %fusion.111.routes, bf16[224,32,128]{2,1,0:T(8,128)(2,1)} %get-tuple-element.201.held, bf16[512,32,128]{2,1,0:T(8,128)(2,1)} %get-tuple-element.202.results, ...), custom_call_target="tpu_custom_call" | custom-call | tf_op jit(solution)/shard_map/cond/branch_0_fun/exchange/pallas_call | solution.py:233
  174.0 15.3 %collocate.1 = (f32[8,1,1024]{2,1,0:T(1,128)}, bf16[120,64,64]{2,1,0:T(8,128)(2,1)}, bf16[120,64,64]{2,1,0:T(8,128)(2,1)}) custom-call(s32[512]{0:T(512)} %reshape.489.label, s32[120]{0:T(128)} %broadcast_select_fusion.place, bf16[512,32,128]{2,1,0:T(8,128)(2,1)} %get-tuple-element.224.blocks, bf16[8,512,1024]{2,1,0:T(8,128)(2,1)} %bitcast.111, ...), custom_call_target="tpu_custom_call" | custom-call | tf_op jit(solution)/shard_map/collocate/pallas_call | solution.py:558
  (14 shorter events, 0.2 us)
Async XLA Ops:
  40.9 12.4 %copy-start = (bf16[24,5,64,64]{3,2,1,0:T(8,128)(2,1)S(1)}, bf16[24,5,64,64]{3,2,1,0:T(8,128)(2,1)}, u32[]{:S(2)}) copy-start(bf16[24,5,64,64]{3,2,1,0:T(8,128)(2,1)} %param.9) | copy-start | bytes 2949124

commit v5 on v4

--- a/solution.py
+++ b/solution.py
@@ -82,8 +82,8 @@
 
 
 def exchange_kernel(
-    inverse, routes, held, results, density, margin, arrived, back, product,
-    zgot, pgot, zput, pput, dens, marg, even, odd, zs, zr, ps, pr, zs2, zr2, ps2, pr2, hs, hr, own,
+    inverse, routes, picks, held, results, density, margin, arrived, back, product,
+    table, chosen, zgot, pgot, zput, pput, dens, marg, even, odd, zs, zr, ps, pr, zs2, zr2, ps2, pr2, hs, hr, own,
 ):
     row, col = lax.axis_index("row"), lax.axis_index("col")
     y, x, high = row // 8, lax.rem(row // 2, 4), lax.rem(row, 2)
@@ -125,6 +125,7 @@
         pl.semaphore_signal(barrier, inc=1, device_id=across(steps)[1], device_id_type=MESH)
     for where in (after, before):
         pl.semaphore_signal(barrier, inc=1, device_id=where, device_id_type=MESH)
+    filled = keep(results, table, own.at[6])
     loads = [keep(density, dens, own.at[0]), keep(margin, marg.at[pl.ds(2, 24)], own.at[1])]
     pl.semaphore_wait(barrier, len(ZSTEPS) + len(PSTEPS) + 2)
 
@@ -133,14 +134,32 @@
         send(margin.at[pl.ds(0, 2)], marg.at[pl.ds(26, 2)], hs.at[1], hr.at[1], before),
     ]
     first_z, first_p = [], []
-    for number in range(len(PSTEPS)):
-        if number < len(ZSTEPS):
-            to, where = along(ZSTEPS[number])
-            first_z.append(send(rows(held, to, CAP), rows(zgot, z, CAP), zs.at[number], zr.at[number], where))
+    for number in range(len(ZSTEPS)):
+        to, where = along(ZSTEPS[number])
+        first_z.append(send(rows(held, to, CAP), rows(zgot, z, CAP), zs.at[number], zr.at[number], where))
+    own_z = keep(rows(held, z, CAP), rows(zgot, z, CAP), own.at[2])
+    filled.wait()
+
+    def gather_source(to):
+        def body(step, carry):
+            for inner in range(8):
+                spot = to * 16 + step * 8 + inner
+                chosen[spot] = table[picks[spot]]
+            return carry
+
+        lax.fori_loop(0, 2, body, 0)
+
+    def source(number):
         to, where = across(PSTEPS[number])
-        first_p.append(send(rows(results, to, 16), rows(pgot, here, 16), ps.at[number], pr.at[number], where))
-    own_z = keep(rows(held, z, CAP), rows(zgot, z, CAP), own.at[2])
-    own_p = keep(rows(results, here, 16), rows(pgot, here, 16), own.at[3])
+        return send(rows(chosen, to, 16), rows(pgot, here, 16), ps.at[number], pr.at[number], where)
+
+    gather_source(across(PSTEPS[0])[0])
+    for number in range(1, len(PSTEPS)):
+        gather_source(across(PSTEPS[number])[0])
+        first_p.append(source(number - 1))
+    gather_source(here)
+    first_p.append(source(len(PSTEPS) - 1))
+    own_p = keep(rows(chosen, here, 16), rows(pgot, here, 16), own.at[3])
 
     def clear(atom, carry):
         even[atom] = jnp.zeros((BF, WIDE), jnp.bfloat16)
@@ -227,7 +246,7 @@
         copy.wait()
 
 
-def exchanged(inverse, routes, held, results, density, margin):
+def exchanged(inverse, routes, picks, held, results, density, margin):
     hbm = pl.BlockSpec(memory_space=pl.ANY)
     dma = pltpu.SemaphoreType.DMA
     return pl.pallas_call(
@@ -237,9 +256,11 @@
             jax.ShapeDtypeStruct((HELD, ROWS, LANES), jnp.bfloat16),
             jax.ShapeDtypeStruct((24, BF, 384), jnp.bfloat16),
         ),
-        in_specs=[SMEM, SMEM, hbm, hbm, hbm, hbm],
+        in_specs=[SMEM, SMEM, SMEM, hbm, hbm, hbm, hbm],
         out_specs=(hbm, hbm, VM),
         scratch_shapes=[
+            pltpu.VMEM((SLOTS_ALL, ROWS, LANES), jnp.bfloat16),
+            pltpu.VMEM((SLOTS_ALL, ROWS, LANES), jnp.bfloat16),
             pltpu.VMEM((HELD, ROWS, LANES), jnp.bfloat16),
             pltpu.VMEM((SLOTS_ALL, ROWS, LANES), jnp.bfloat16),
             pltpu.VMEM((HELD, ROWS, LANES), jnp.bfloat16),
@@ -250,11 +271,11 @@
             pltpu.VMEM((28, BF, WIDE), jnp.bfloat16),
             dma((7,)), dma((7,)), dma((31,)), dma((31,)),
             dma((7,)), dma((7,)), dma((31,)), dma((31,)),
-            dma((2,)), dma((2,)), dma((6,)),
+            dma((2,)), dma((2,)), dma((7,)),
         ],
         compiler_params=params(collective_id=0, has_side_effects=True),
         name="exchange",
-    )(inverse, routes, held, results, density, margin)
+    )(inverse, routes, picks, held, results, density, margin)
 
 
 def notice_kernel(
@@ -349,8 +370,7 @@
     )(which, table, potential, flat)
 
 
-def matrix_kernel(label, basis, potential, out, scaled, table):
-    task = pl.program_id(0)
+def matrix_kernel(basis, potential, table, scaled):
     phi = basis[0]
     scaled[...] = (phi.astype(jnp.float32) * potential[0]).astype(jnp.bfloat16)
     full = lax.dot_general(
@@ -362,19 +382,9 @@
             columns = slice(pair * LANES, (pair + 1) * LANES)
             top = full[first * BF : first * BF + ROWS, columns]
             low = full[first * BF + ROWS : (first + 1) * BF, columns]
-            spot = task * 64 + first * 8 + 2 * pair
+            spot = first * 8 + 2 * pair
             table[spot] = jnp.where(left, top, pltpu.roll(low, BF, 1)).astype(jnp.bfloat16)
             table[spot + 1] = jnp.where(left, pltpu.roll(top, BF, 1), low).astype(jnp.bfloat16)
-
-    @pl.when(task == TASKS - 1)
-    def _():
-        def body(step, carry):
-            for inner in range(16):
-                slot = step * 16 + inner
-                out[slot] = table[jnp.maximum(label[slot], 0)]
-            return carry
-
-        lax.fori_loop(0, SLOTS_ALL // 16, body, 0)
 
 
 def grid_kernel(label, place, blocks, basis, back, product, out, ks, margins, table, weights):
@@ -523,24 +533,22 @@
         out_shape=BLOCKS,
         grid=(TASKS,),
         in_specs=[
-            SMEM,
             pl.BlockSpec((1, BASIS, POINTS), lambda t: (t, 0, 0)),
             pl.BlockSpec((1, 1, POINTS), lambda t: (t, 0, 0)),
         ],
-        out_specs=whole(BLOCKS.shape),
-        scratch_shapes=[
-            pltpu.VMEM((BASIS, POINTS), jnp.bfloat16),
-            pltpu.VMEM((SLOTS_ALL, ROWS, LANES), jnp.bfloat16),
-        ],
+        out_specs=pl.BlockSpec((64, ROWS, LANES), lambda t: (t, 0, 0)),
+        scratch_shapes=[pltpu.VMEM((BASIS, POINTS), jnp.bfloat16)],
         compiler_params=params(),
         cost_estimate=pl.CostEstimate(flops=2 * TASKS * BASIS * BASIS * POINTS, bytes_accessed=14 << 20, transcendentals=0),
         name="matrices",
-    )(labels, phi, box_potential)
-
-    def fast(results, held, density, margin, places, routes, inverse):
-        return exchanged(inverse, routes, held, results, density, margin)
-
-    def dense(results, held, density, margin, places, routes, inverse):
+    )(phi, box_potential)
+    picks = jnp.maximum(labels, 0)
+
+    def fast(results, held, density, margin, places, routes, inverse, picks):
+        return exchanged(inverse, routes, picks, held, results, density, margin)
+
+    def dense(results, held, density, margin, places, routes, inverse, picks):
+        results = results[picks]
         outgoing = packed(places, density.reshape(PAIRS, BF, BF), SLOTS_ALL)
         arrived = by_plane(lax.all_to_all(outgoing.reshape(PEERS, 64, LANES), ALL, 0, 0, tiled=True))
         returned = lax.all_to_all(by_mesh(results.reshape(PEERS, 64, LANES)), ALL, 0, 0, tiled=True)
@@ -552,7 +560,7 @@
             jnp.pad(wide, ((0, 0), (0, 0), (0, BF))),
         )
 
-    arrived, back, product = lax.cond(over, dense, fast, results, held, density, margin, places, routes, inverse)
+    arrived, back, product = lax.cond(over, dense, fast, results, held, density, margin, places, routes, inverse, picks)
     pickup = jnp.where(over, jnp.arange(PAIRS, dtype=jnp.int32), spots)
 
     grid_rows, ks_blocks, margin_product = pl.pallas_call(

time: 192 us -> 190 us (0.990)
  no operation moved by 1% of the time
where the time goes in v5:
time: 190 us; the launch traced here: 187 us
  Pallas kernels  172 us (91%)
  other arithmetic  6.54 us (3%)
  local copies, waits for them, and re-layouts  5.39 us (3%)
  between operations  2.11 us (1%)
    pallas_call x1, Pallas kernels, exchanged(): pl.pallas_call(exchange_kernel, out_shape=(BLOCKS, jax.ShapeDtypeStruct((...  118 us
    pallas_call x1, Pallas kernels, noticed(): pl.pallas_call(notice_kernel, out_shape=(jax.ShapeDtypeStruct((PLANE, ZS,...  26.7 us
    pallas_call x1, Pallas kernels, local(): pl.pallas_call(grid_kernel, out_shape=(jax.ShapeDtypeStruct((TASKS, 1, PO...  15.7 us
    pallas_call x1, Pallas kernels, local(): pl.pallas_call(matrix_kernel, out_shape=BLOCKS, grid=(TASKS,), in_specs=[...  10.8 us

profile of v5, /device:TPU:1, one launch (start us, length us, event | category | flops | bytes accessed | tf_op | source)
XLA Modules:
  0.0 187.2 jit_solution(2652083154494751175)
XLA Ops:
  0.7 0.8 fusion.149
  1.5 0.1 copy.42
  1.6 0.1 broadcast_in_dim.137
  1.7 0.1 copy.43
  1.8 0.1 broadcast_in_dim.139
  1.9 0.8 copy.40
  2.7 0.1 reshape.484
  2.8 0.2 convert_reduce_fusion
  3.0 0.2 convert_reduce_fusion.1
  3.2 0.6 fusion.150
  4.5 0.7 select_reduce_fusion.1.which
  5.1 0.8 copy.41
  5.9 0.1 broadcast_in_dim.134
  6.0 1.4 reshape.486.potential
  7.4 0.3 fusion.117
  7.7 0.9 fusion.114
  8.7 26.7 %notices.1 = (s32[32,8,1,128]{3,2,1,0:T(1,128)}, f32[32,1,256]{2,1,0:T(1,128)}, bf16[224,32,128]{2,1,0:T(8,128)(2,1)}) custom-call(s32[224]{0:T(256)} %select_reduce_fusion.1.which, s32[8,32,1,128]{3,2,1,0:T(1,128)} %bitcast.118, f32[32,1,256]{2,1,0:T(1,128)} %reshape.486.potential, bf16[120,64,64]{2,1,0:T(8,128)(2,1)} %bitcast.105), custom_call_target="tpu_custom_call" | custom-call | tf_op jit(solution)/shard_map/notices/pallas_call | solution.py:354
  35.4 1.6 slice_reduce_fusion
  37.7 0.6 broadcast_select_fusion.place
  38.2 0.8 constant_dynamic-slice_fusion
  39.0 1.2 fusion.115
  40.2 0.1 reshape.489.label
  40.3 0.0 copy-start.4
  40.3 0.0 copy-start
  40.3 10.8 %matrices.1 = bf16[512,32,128]{2,1,0:T(8,128)(2,1)} custom-call(bf16[8,512,1024]{2,1,0:T(8,128)(2,1)} %bitcast.110, f32[8,1,1024]{2,1,0:T(1,128)} %bitcast.122), custom_call_target="tpu_custom_call" | custom-call | flops 4294967296 | bytes 14680064 | tf_op jit(solution)/shard_map/matrices/pallas_call | solution.py:531
  51.1 0.0 copy-done.4
  51.1 0.0 copy-done
  51.2 120.3 %conditional.1 = ((bf16[512,32,128]{2,1,0:T(8,128)(2,1)}, bf16[224,32,128]{2,1,0:T(8,128)(2,1)}, bf16[24,64,384]{2,1,0:T(8,128)(2,1)S(1)})) conditional(s32[]{:T(128)} %convert_element_type.34, (s32[8,28]{1,0:T(8,128)S(1)}, (), s32[]{:T(128)}, s32[1,224]{1,0:T(1,128)S(1)}, s32[512,224]{1,0:T(8,128)S(1)}, /*index=5*/s32[512,224]{1,0:T(8,128)S(1)}, ...), branch_computations={%region_5.7_spmd, %region_7.8_spmd} | conditional | flops 250876000 | bytes 119540808 | solution.py:563
  51.2 0.1 reshape.520
  51.3 0.8 select_reduce_fusion.inverse
  52.1 0.1 reshape.521
  52.1 0.6 fusion.111.routes
  52.7 118.5 %exchange.1 = (bf16[512,32,128]{2,1,0:T(8,128)(2,1)}, bf16[224,32,128]{2,1,0:T(8,128)(2,1)}, bf16[24,64,384]{2,1,0:T(8,128)(2,1)S(1)}) custom-call(s32[512]{0:T(512)} %select_reduce_fusion.inverse, s32[224]{0:T(256)} %fusion.111.routes, s32[512]{0:T(512)S(1)} %get-tuple-element.211.picks, bf16[224,32,128]{2,1,0:T(8,128)(2,1)} %get-tuple-element.212.held, ...), custom_call_target="tpu_custom_call" | custom-call | tf_op jit(solution)/shard_map/cond/branch_0_fun/exchange/pallas_call | solution.py:252
  171.4 15.7 %collocate.1 = (f32[8,1,1024]{2,1,0:T(1,128)}, bf16[120,64,64]{2,1,0:T(8,128)(2,1)}, bf16[120,64,64]{2,1,0:T(8,128)(2,1)}) custom-call(s32[512]{0:T(512)} %copy-done.4, s32[120]{0:T(128)} %broadcast_select_fusion.place, bf16[512,32,128]{2,1,0:T(8,128)(2,1)} %get-tuple-element.237.blocks, bf16[8,512,1024]{2,1,0:T(8,128)(2,1)} %bitcast.111, ...), custom_call_target="tpu_custom_call" | custom-call | tf_op jit(solution)/shard_map/collocate/pallas_call | solution.py:566
  (15 shorter events, 0.2 us)
Async XLA Ops:
  40.3 10.8 %copy-start.4 = (s32[512]{0:T(512)}, s32[512]{0:T(512)S(1)}, u32[]{:S(2)}) copy-start(s32[512]{0:T(512)S(1)} %reshape.489.label) | copy-start | bytes 6148
  40.3 10.8 %copy-start = (bf16[24,5,64,64]{3,2,1,0:T(8,128)(2,1)S(1)}, bf16[24,5,64,64]{3,2,1,0:T(8,128)(2,1)}, u32[]{:S(2)}) copy-start(bf16[24,5,64,64]{3,2,1,0:T(8,128)(2,1)} %param.9) | copy-start | bytes 2949124
